TPU v7x, 256 devices: a whole 4x4x8 slice. The times are simulated.
256 devices in a mesh: dp: 8 (over x, core), expert: 32 (over y, z).
Axes of the slice: x: 4, y: 4, z: 8, core: 2. Of those that a mesh axis runs over, the one named last changes fastest.
Arguments:
- tokens: bfloat16 [6144, 2048], P(('dp', 'expert')), may hold values from -6 to 6
- out_grad: bfloat16 [6144, 2048], P(('dp', 'expert')), may hold values from -0.59765625 to 0.59765625
- expert_ids: int32 [6144, 8], P(('dp', 'expert')), may hold values from 0 to 31, all different within a row; in each aligned block of 24 rows (0 to 23, 24 to 47, ...) at most 8 rows name the same one
- router_weight: bfloat16 [2048, 32], replicated, may hold values from -0.1875 to 0.1875
- w_gate: bfloat16 [32, 2048, 768], P('expert'), may hold values from -0.125 to 0.125
- w_up: bfloat16 [32, 2048, 768], P('expert'), may hold values from -0.125 to 0.125
- w_down: bfloat16 [32, 768, 2048], P('expert'), may hold values from -0.21875 to 0.21875
Outputs:
- grad_tokens: bfloat16 [6144, 2048], P(('dp', 'expert'))
- grad_router: float32 [2048, 32], replicated
- grad_gate: bfloat16 [32, 2048, 768], P('expert', 'dp')
- grad_up: bfloat16 [32, 2048, 768], P('expert', 'dp')
- grad_down: bfloat16 [32, 768, 2048], P('expert', 'dp')
Inputs may be any that keep to these rules, and one draw needn't show every extreme that they name: `expert_ids`: each row names 8 different experts. Among the 24 tokens of one device (aligned blocks of rows), no expert is named by more than 8 tokens, and in some blocks one expert is named by exactly 8.
All inputs are finite; a program needn't handle non-finite values.
Results may differ from a plain program's by a relative error of at most 0.017.
Values may be sent and summed in bfloat16 or wider, within the bound.
A program may use at most 128 MiB of HBM per device.

v0:
```python
import jax
import jax.numpy as jnp
from jax import lax
from jax.sharding import PartitionSpec as P

PASSES = 3


def expert_rows(rows_in, rows_grad, weight_gate, weight_up, weight_down):
    gate_pre = jnp.dot(rows_in, weight_gate, preferred_element_type=jnp.float32)
    up_pre = jnp.dot(rows_in, weight_up, preferred_element_type=jnp.float32)
    sigmoid_gate = jax.nn.sigmoid(gate_pre)
    activation = gate_pre * sigmoid_gate
    hidden = activation * up_pre
    contract_cols = (((1,), (1,)), ((), ()))
    hidden_grad = lax.dot_general(
        rows_grad, weight_down, contract_cols, preferred_element_type=jnp.float32
    )
    score_grad = jnp.sum(hidden_grad * hidden, axis=1).astype(jnp.bfloat16)
    gate_grad = (
        hidden_grad * up_pre * sigmoid_gate * (1.0 + gate_pre * (1.0 - sigmoid_gate))
    ).astype(jnp.bfloat16)
    up_grad = (hidden_grad * activation).astype(jnp.bfloat16)
    input_grad = lax.dot_general(
        gate_grad, weight_gate, contract_cols, preferred_element_type=jnp.float32
    )
    input_grad = input_grad + lax.dot_general(
        up_grad, weight_up, contract_cols, preferred_element_type=jnp.float32
    )
    return (
        hidden.astype(jnp.bfloat16),
        gate_grad,
        up_grad,
        input_grad.astype(jnp.bfloat16),
        score_grad,
    )


def scaled_rows(gate_values, rows_grad, gate_grad, up_grad):
    gate_scale = gate_values.astype(jnp.float32)[:, None]
    return (
        (gate_scale * rows_grad).astype(jnp.bfloat16),
        (gate_scale * gate_grad).astype(jnp.bfloat16),
        (gate_scale * up_grad).astype(jnp.bfloat16),
    )


def balancer_forward_pass(router_logit_rows):
    expert_density_rows = [jnp.exp(router_logit_rows)]
    division_ratios, column_totals, row_totals = ([], [], [])
    for repeat in range(PASSES):
        column_sum = lax.psum(jnp.sum(expert_density_rows[-1], axis=0), ("dp", "expert"))
        quotient = expert_density_rows[-1] / column_sum
        row_sum = jnp.sum(quotient, axis=1, keepdims=True)
        expert_density_rows.append(quotient / row_sum)
        division_ratios.append(quotient)
        column_totals.append(column_sum)
        row_totals.append(row_sum)
    return (expert_density_rows, division_ratios, column_totals, row_totals)


def balancer_adjoint_pass(
    density_gradient, expert_density_rows, division_ratios, column_totals, row_totals
):
    for repeat in reversed(range(PASSES)):
        density = expert_density_rows[repeat + 1]
        quotient_grad = (
            density_gradient - jnp.sum(density_gradient * density, axis=1, keepdims=True)
        ) / row_totals[repeat]
        shared = lax.psum(
            jnp.sum(quotient_grad * division_ratios[repeat], axis=0), ("dp", "expert")
        )
        density_gradient = (quotient_grad - shared) / column_totals[repeat]
    return density_gradient * expert_density_rows[0]


def column_product(operand_left, operand_right):
    return lax.dot_general(
        operand_left, operand_right, (((0,), (0,)), ((), ())), preferred_element_type=jnp.float32
    )


def per_device(tokens, out_grad, expert_ids, router_weight, w_gate, w_up, w_down):
    tok_rows, model_width = tokens.shape
    expert_blocks = router_weight.shape[1]
    top_picks = expert_ids.shape[1]
    capacity = min(tok_rows, 4 * tok_rows * top_picks // (3 * expert_blocks))
    sources = lax.axis_size("expert")
    slot_total = sources * capacity
    weight_gate, weight_up, weight_down = (w_gate[0], w_up[0], w_down[0])
    ff_width = weight_gate.shape[1]
    highest = lax.Precision.HIGHEST
    router_logit_rows = jnp.dot(tokens, router_weight, preferred_element_type=jnp.float32)
    expert_range = jnp.arange(expert_blocks, dtype=jnp.int32)
    picked = jnp.sum(
        (expert_ids[:, :, None] == expert_range[None, None, :]).astype(jnp.int32), axis=1
    )
    slot_rank = jnp.cumsum(picked, axis=0) - picked
    slot_range = jnp.arange(capacity, dtype=jnp.int32)
    selected = (slot_rank.T[:, None, :] == slot_range[None, :, None]) & (picked.T[:, None, :] > 0)
    select_half = selected.astype(jnp.bfloat16)
    select_full = selected.astype(jnp.float32)
    send_in = jnp.einsum(
        "ect,td->ecd", select_half, tokens, preferred_element_type=jnp.float32
    ).astype(jnp.bfloat16)
    send_grad = jnp.einsum(
        "ect,td->ecd", select_half, out_grad, preferred_element_type=jnp.float32
    ).astype(jnp.bfloat16)
    balancer_state = balancer_forward_pass(router_logit_rows)
    gate_matrix = expert_blocks * balancer_state[0][-1]
    send_gates = jnp.einsum("ect,te->ec", select_full, gate_matrix, precision=highest).astype(
        jnp.bfloat16
    )
    recv_in, recv_grad, recv_gates = (
        lax.all_to_all(send_in, "expert", split_axis=0, concat_axis=0, tiled=True),
        lax.all_to_all(send_grad, "expert", split_axis=0, concat_axis=0, tiled=True),
        lax.all_to_all(send_gates, "expert", split_axis=0, concat_axis=0, tiled=True),
    )
    flat_in = recv_in.reshape(slot_total, model_width)
    flat_grad = recv_grad.reshape(slot_total, model_width)
    hidden, gate_grad, up_grad, input_grad, score_grad = expert_rows(
        flat_in, flat_grad, weight_gate, weight_up, weight_down
    )
    input_slots, score_slots = (input_grad, score_grad)
    back_input, back_score = (
        lax.all_to_all(
            input_slots.reshape(sources, capacity, model_width),
            "expert",
            split_axis=0,
            concat_axis=0,
            tiled=True,
        ),
        lax.all_to_all(
            score_slots.reshape(sources, capacity),
            "expert",
            split_axis=0,
            concat_axis=0,
            tiled=True,
        ),
    )
    gate_values = recv_gates.reshape(slot_total)
    down_scaled, gate_scaled, up_scaled = scaled_rows(gate_values, flat_grad, gate_grad, up_grad)
    paired = jnp.concatenate([gate_scaled, up_scaled], axis=1)
    grad_pair = lax.psum_scatter(
        column_product(flat_in, paired).astype(jnp.bfloat16), "dp", scatter_dimension=0, tiled=True
    ).astype(jnp.float32)
    grad_down = lax.psum_scatter(
        column_product(hidden, down_scaled).astype(jnp.bfloat16),
        "dp",
        scatter_dimension=0,
        tiled=True,
    ).astype(jnp.float32)
    grad_gate = grad_pair[:, :ff_width].astype(jnp.bfloat16)[None]
    grad_up = grad_pair[:, ff_width:].astype(jnp.bfloat16)[None]
    grad_down = grad_down.astype(jnp.bfloat16)[None]
    route_weights = select_full * gate_matrix.T[:, None, :]
    expert_input = jnp.einsum(
        "ect,ecd->td", route_weights, back_input.astype(jnp.float32), precision=highest
    )
    density_gradient = expert_blocks * jnp.einsum(
        "ect,ec->te", select_full, back_score.astype(jnp.float32), precision=highest
    )
    expert_density_rows, division_ratios, column_totals, row_totals = balancer_state
    logit_gradient = balancer_adjoint_pass(
        density_gradient, expert_density_rows, division_ratios, column_totals, row_totals
    ).astype(jnp.bfloat16)
    router_term = lax.dot_general(
        tokens, logit_gradient, (((0,), (0,)), ((), ())), preferred_element_type=jnp.float32
    )
    grad_router = lax.psum(router_term, ("dp", "expert"))
    router_input = lax.dot_general(
        logit_gradient, router_weight, (((1,), (1,)), ((), ())), preferred_element_type=jnp.float32
    )
    grad_tokens = (expert_input + router_input).astype(jnp.bfloat16)
    return (grad_tokens, grad_router, grad_gate, grad_up, grad_down)


def solution(mesh):
    in_specs = (
        P(("dp", "expert"), None),
        P(("dp", "expert"), None),
        P(("dp", "expert"), None),
        P(),
        P("expert", None, None),
        P("expert", None, None),
        P("expert", None, None),
    )
    out_specs = (
        P(("dp", "expert"), None),
        P(),
        P("expert", "dp", None),
        P("expert", "dp", None),
        P("expert", "dp", None),
    )
    return jax.shard_map(
        per_device, mesh=mesh, in_specs=in_specs, out_specs=out_specs, check_vma=False
    )
```

profile of v0, /device:TPU:1, one launch (start us, length us, event | category | flops | bytes accessed | tf_op | source)
XLA Modules:
  0.0 830.3 jit_solution(2231783137656285111)
XLA Ops:
  8.0 0.9 copy.34
  9.0 0.1 convert_reduce_fusion
  9.1 1.1 fusion.58
  10.2 81.4 %psum.49 = f32[32]{0:T(128)S(1)} all-reduce(f32[32]{0:T(128)S(1)} %get-tuple-element.16), channel_id=1, replica_groups=mesh['dp'=8,'expert'=32] {'dp','expert'}, use_global_device_ids=true, to_apply=%region_3.4 | all-reduce | flops 32 | bytes 256 | tf_op jit(solution)/shard_map/psum | solution.py:52
  91.6 0.1 fusion.49
  91.7 0.1 fusion.50
  91.9 72.4 %psum.50 = f32[32]{0:T(128)S(1)} all-reduce(f32[32]{0:T(128)S(1)} %fusion.50), channel_id=1, replica_groups=mesh['dp'=8,'expert'=32] {'dp','expert'}, use_global_device_ids=true, to_apply=%region_6.7 | all-reduce | flops 32 | bytes 256 | tf_op jit(solution)/shard_map/psum | solution.py:52
  164.3 0.2 fusion.53
  164.5 0.1 fusion.54
  164.6 73.7 %psum.51 = f32[32]{0:T(128)S(1)} all-reduce(f32[32]{0:T(128)S(1)} %fusion.54), channel_id=1, replica_groups=mesh['dp'=8,'expert'=32] {'dp','expert'}, use_global_device_ids=true, to_apply=%region_9.10 | all-reduce | flops 32 | bytes 256 | tf_op jit(solution)/shard_map/psum | solution.py:52
  238.3 0.2 fusion.55
  238.6 0.7 copy.40
  239.3 6.3 all-to-all-start.4
  245.6 0.1 copy.35
  245.7 2.3 convolution_convert_fusion.2
  248.0 6.1 all-to-all-done.4
  254.2 4.7 all-to-all-start.1
  258.9 1.4 convolution_convert_fusion.3
  260.3 23.0 %all-to-all-done.1 = bf16[32,8,2048]{2,1,0:T(8,128)(2,1)} async-done(((bf16[32,8,2048]{2,1,0:T(8,128)(2,1)}), bf16[32,8,2048]{2,1,0:T(8,128)(2,1)}, u32[]{:S(2)}, u32[]{:S(2)}) %all-to-all-start.1) | async-done | bytes 1048608 | tf_op jit(solution)/shard_map/all_to_all | solution.py:115
  283.3 8.3 all-to-all-start
  291.8 4.1 fusion.6
  295.9 20.2 %all-to-all-done = bf16[32,8,2048]{2,1,0:T(8,128)(2,1)} async-done(((bf16[32,8,2048]{2,1,0:T(8,128)(2,1)}), bf16[32,8,2048]{2,1,0:T(8,128)(2,1)}, u32[]{:S(2)}, u32[]{:S(2)}) %all-to-all-start) | async-done | bytes 1048608 | tf_op jit(solution)/shard_map/all_to_all | solution.py:116
  316.1 3.3 fusion.8
  319.4 3.6 multiply_convert_fusion.3
  323.1 5.7 convolution_convert_fusion
  328.9 0.1 convert_element_type.110
  329.0 16.5 %all_to_all.33 = bf16[32,1,8]{2,1,0:T(2,128)(2,1)S(1)} all-to-all(bf16[32,1,8]{2,1,0:T(2,128)(2,1)S(1)} %convert_element_type.110), channel_id=1, replica_groups=mesh['dp'=8,'expert'=32] {'expert'}, dimensions={0} | all-to-all | bytes 1024 | tf_op jit(solution)/shard_map/all_to_all | solution.py:133
  345.6 0.2 fusion.46
  345.8 0.1 multiply_reduce_fusion.5
  345.9 75.5 %psum.52 = f32[32]{0:T(128)S(1)} all-reduce(f32[32]{0:T(128)S(1)} %multiply_reduce_fusion.5), channel_id=1, replica_groups=mesh['dp'=8,'expert'=32] {'dp','expert'}, use_global_device_ids=true, to_apply=%region_14.15 | all-reduce | flops 32 | bytes 256 | tf_op jit(solution)/shard_map/psum | solution.py:70
  421.4 0.2 multiply_reduce_fusion.4
  421.6 0.1 multiply_reduce_fusion.3
  421.7 73.7 %psum.53 = f32[32]{0:T(128)S(1)} all-reduce(f32[32]{0:T(128)S(1)} %get-tuple-element.9), channel_id=1, replica_groups=mesh['dp'=8,'expert'=32] {'dp','expert'}, use_global_device_ids=true, to_apply=%region_17.18 | all-reduce | flops 32 | bytes 256 | tf_op jit(solution)/shard_map/psum | solution.py:70
  495.4 0.2 multiply_reduce_fusion.2
  495.6 0.1 multiply_reduce_fusion.1
  495.7 73.5 %psum.54 = f32[32]{0:T(128)S(1)} all-reduce(f32[32]{0:T(128)S(1)} %multiply_reduce_fusion.1), channel_id=1, replica_groups=mesh['dp'=8,'expert'=32] {'dp','expert'}, use_global_device_ids=true, to_apply=%region_20.21 | all-reduce | flops 32 | bytes 256 | tf_op jit(solution)/shard_map/psum | solution.py:70
  569.2 1.0 convolution_bitcast_fusion
  570.3 4.6 convolution_convert_fusion.1
  574.9 0.9 copy-done.5
  575.9 1.0 fusion
  577.0 2.0 fusion.16
  579.0 6.3 all-to-all-start.2
  585.5 24.8 %all-to-all-done.2 = bf16[32,8,2048]{2,1,0:T(8,128)(2,1)} async-done(((bf16[32,8,2048]{2,1,0:T(8,128)(2,1)}), bf16[32,8,2048]{2,1,0:T(8,128)(2,1)}, u32[]{:S(2)}, u32[]{:S(2)}) %all-to-all-start.2) | async-done | bytes 1048608 | tf_op jit(solution)/shard_map/all_to_all | solution.py:126
  610.3 2.4 convolution_bitcast_fusion.1
  612.7 0.9 fusion.19
  613.6 2.0 slice_bitcast_fusion
  615.6 205.5 %all-reduce.2.cloned.1.call-done = f32[2048,32]{0,1:T(8,128)} async-done(((f32[2048,32]{0,1:T(8,128)}), f32[2048,32]{0,1:T(8,128)}) %all-reduce.2.cloned.1.call-update) | async-done | bytes 262160 | tf_op jit(solution)/shard_map/psum | solution.py:170
  821.2 1.7 copy.56
  (79 shorter events, 0.9 us)
Async XLA Ops:
  8.0 311.4 %copy-start = (bf16[1,2048,768]{2,1,0:T(8,128)(2,1)S(1)}, bf16[1,2048,768]{2,1,0:T(8,128)(2,1)}, u32[]{:S(2)}) copy-start(bf16[1,2048,768]{2,1,0:T(8,128)(2,1)} %param.11) | copy-start | bytes 9437188
  8.0 250.9 %copy-start.12 = (bf16[24,2048]{1,0:T(8,128)(2,1)S(1)}, bf16[24,2048]{1,0:T(8,128)(2,1)}, u32[]{:S(2)}) copy-start(bf16[24,2048]{1,0:T(8,128)(2,1)} %param.8) | copy-start | bytes 294916
  91.7 477.4 %copy-start.10 = (f32[24]{0:T(128)}, f32[24]{0:T(128)S(1)}, u32[]{:S(2)}) copy-start(f32[24]{0:T(128)S(1)} %fusion.49) | copy-start | bytes 292
  91.9 253.7 %copy-start.8 = (s32[32,24]{0,1:T(8,128)}, s32[32,24]{0,1:T(8,128)S(1)}, u32[]{:S(2)}) copy-start(s32[32,24]{0,1:T(8,128)S(1)} %subtract_bitcast_fusion) | copy-start | bytes 9220
  164.3 404.9 %copy-start.13 = (f32[32]{0:T(128)}, f32[32]{0:T(128)S(1)}, u32[]{:S(2)}) copy-start(f32[32]{0:T(128)S(1)} %psum.50) | copy-start | bytes 388
  164.5 257.1 %copy-start.17 = (f32[24]{0:T(128)}, f32[24]{0:T(128)S(1)}, u32[]{:S(2)}) copy-start(f32[24]{0:T(128)S(1)} %fusion.53) | copy-start | bytes 292
  164.6 181.0 %copy-start.15 = (pred[32,24]{0,1:T(8,128)(4,1)}, pred[32,24]{0,1:T(8,128)(4,1)S(1)}, u32[]{:S(2)}) copy-start(pred[32,24]{0,1:T(8,128)(4,1)S(1)} %compare_bitcast_fusion) | copy-start | bytes 2308
  238.3 183.3 %copy-start.19 = (f32[32]{0:T(128)}, f32[32]{0:T(128)S(1)}, u32[]{:S(2)}) copy-start(f32[32]{0:T(128)S(1)} %psum.51) | copy-start | bytes 388
  238.4 183.2 %copy-start.21 = (f32[24]{0:T(128)}, f32[24]{0:T(128)S(1)}, u32[]{:S(2)}) copy-start(f32[24]{0:T(128)S(1)} %fusion.55) | copy-start | bytes 292
  239.3 14.9 %all-to-all-start.4 = ((bf16[32,1,8]{2,1,0:T(2,128)(2,1)}), bf16[32,1,8]{2,1,0:T(2,128)(2,1)S(1)}, u32[]{:S(2)}, u32[]{:S(2)}) async-start(bf16[32,1,8]{2,1,0:T(2,128)(2,1)} %copy.40), calls=%async_computation.4 | async-start | bytes 32768 | tf_op jit(solution)/shard_map/all_to_all | solution.py:117
  254.2 29.1 %all-to-all-start.1 = ((bf16[32,8,2048]{2,1,0:T(8,128)(2,1)}), bf16[32,8,2048]{2,1,0:T(8,128)(2,1)}, u32[]{:S(2)}, u32[]{:S(2)}) async-start(bf16[32,8,2048]{2,1,0:T(8,128)(2,1)} %convolution_convert_fusion.2), calls=%async_computation.1 | async-start | bytes 2097152 | tf_op jit(solution)/shard_map/all_to_all | solution.py:115
  283.3 32.8 %all-to-all-start = ((bf16[32,8,2048]{2,1,0:T(8,128)(2,1)}), bf16[32,8,2048]{2,1,0:T(8,128)(2,1)}, u32[]{:S(2)}, u32[]{:S(2)}) async-start(bf16[32,8,2048]{2,1,0:T(8,128)(2,1)} %convolution_convert_fusion.3), calls=%async_computation | async-start | bytes 2097152 | tf_op jit(solution)/shard_map/all_to_all | solution.py:116
  291.6 322.0 %reduce-scatter.3.cloned.1.call-start = ((), (), s32[]{:S(2)}) async-start(), calls=%async_computation.8 | async-start | bytes 7077888 | tf_op jit(solution)/shard_map/reduce_scatter | solution.py:144
  316.1 3.3 copy-start.29
  328.8 240.4 %copy-start.2 = (bf16[24,2048]{1,0:T(8,128)(2,1)S(1)}, bf16[24,2048]{1,0:T(8,128)(2,1)}, u32[]{:S(2)}) copy-start(bf16[24,2048]{1,0:T(8,128)(2,1)} %param.7) | copy-start | bytes 294916
  328.8 492.3 %all-reduce.2.cloned.1.call-start = ((), (), s32[]{:S(2)}) async-start(), calls=%async_computation.7 | async-start | bytes 524288 | tf_op jit(solution)/shard_map/psum | solution.py:170
  421.7 148.5 %copy-start.6 = (f32[24,32]{1,0:T(8,128)}, f32[24,32]{1,0:T(8,128)S(1)}, u32[]{:S(2)}) copy-start(f32[24,32]{1,0:T(8,128)S(1)} %get-tuple-element.10) | copy-start | bytes 9220
  495.4 74.9 %copy-start.23 = (f32[32]{0:T(128)}, f32[32]{0:T(128)S(1)}, u32[]{:S(2)}) copy-start(f32[32]{0:T(128)S(1)} %psum.53) | copy-start | bytes 388
  495.6 74.7 %copy-start.25 = (f32[24]{0:T(128)}, f32[24]{0:T(128)S(1)}, u32[]{:S(2)}) copy-start(f32[24]{0:T(128)S(1)} %multiply_reduce_fusion.2) | copy-start | bytes 292
  569.2 1.1 copy-start.27
  570.2 251.0 %reduce-scatter.5.cloned.1.call-start = ((), (), s32[]{:S(2)}) async-start(), calls=%async_computation.9 | async-start | bytes 3538944 | tf_op jit(solution)/shard_map/reduce_scatter | solution.py:147
  574.9 1.0 copy-start.5
  574.9 2.0 copy-start.1
  574.9 2.0 copy-start.4
  577.0 8.4 %copy-start.11 = (f32[24]{0:T(128)S(1)}, f32[24]{0:T(128)}, u32[]{:S(2)}) copy-start(f32[24]{0:T(128)} %copy-done.10) | copy-start | bytes 292
  577.0 8.4 %copy-start.14 = (f32[32]{0:T(128)S(1)}, f32[32]{0:T(128)}, u32[]{:S(2)}) copy-start(f32[32]{0:T(128)} %copy-done.13) | copy-start | bytes 388
  577.0 8.4 %copy-start.18 = (f32[24]{0:T(128)S(1)}, f32[24]{0:T(128)}, u32[]{:S(2)}) copy-start(f32[24]{0:T(128)} %copy-done.17) | copy-start | bytes 292
  577.0 8.4 %copy-start.20 = (f32[32]{0:T(128)S(1)}, f32[32]{0:T(128)}, u32[]{:S(2)}) copy-start(f32[32]{0:T(128)} %copy-done.19) | copy-start | bytes 388
  577.0 8.4 %copy-start.22 = (f32[24]{0:T(128)S(1)}, f32[24]{0:T(128)}, u32[]{:S(2)}) copy-start(f32[24]{0:T(128)} %copy-done.21) | copy-start | bytes 292
  577.0 33.3 %copy-start.9 = (s32[32,24]{0,1:T(8,128)S(1)}, s32[32,24]{0,1:T(8,128)}, u32[]{:S(2)}) copy-start(s32[32,24]{0,1:T(8,128)} %copy-done.8) | copy-start | bytes 9220
  577.0 33.3 %copy-start.16 = (pred[32,24]{0,1:T(8,128)(4,1)S(1)}, pred[32,24]{0,1:T(8,128)(4,1)}, u32[]{:S(2)}) copy-start(pred[32,24]{0,1:T(8,128)(4,1)} %copy-done.15) | copy-start | bytes 2308
  579.0 33.6 %copy-start.3 = (bf16[2048,32]{0,1:T(8,128)(2,1)S(1)}, bf16[2048,32]{0,1:T(8,128)(2,1)}, u32[]{:S(2)}) copy-start(bf16[2048,32]{0,1:T(8,128)(2,1)} %param.10) | copy-start | bytes 393220
  579.0 33.6 %copy-start.7 = (f32[24,32]{1,0:T(8,128)S(1)}, f32[24,32]{1,0:T(8,128)}, u32[]{:S(2)}) copy-start(f32[24,32]{1,0:T(8,128)} %copy-done.6) | copy-start | bytes 9220
  579.0 33.7 %copy-start.24 = (f32[32]{0:T(128)S(1)}, f32[32]{0:T(128)}, u32[]{:S(2)}) copy-start(f32[32]{0:T(128)} %copy-done.23) | copy-start | bytes 388
  579.0 33.7 %copy-start.26 = (f32[24]{0:T(128)S(1)}, f32[24]{0:T(128)}, u32[]{:S(2)}) copy-start(f32[24]{0:T(128)} %copy-done.25) | copy-start | bytes 292
  579.0 33.7 %copy-start.28 = (f32[32]{0:T(128)S(1)}, f32[32]{0:T(128)}, u32[]{:S(2)}) copy-start(f32[32]{0:T(128)} %copy-done.27) | copy-start | bytes 388
  579.0 31.2 %all-to-all-start.2 = ((bf16[32,8,2048]{2,1,0:T(8,128)(2,1)}), bf16[32,8,2048]{2,1,0:T(8,128)(2,1)}, u32[]{:S(2)}, u32[]{:S(2)}) async-start(bf16[32,8,2048]{2,1,0:T(8,128)(2,1)} %fusion.16), calls=%async_computation.2 | async-start | bytes 2097152 | tf_op jit(solution)/shard_map/all_to_all | solution.py:126
Sparse Core Ops, SparseCore 0:
  328.9 43.8 reduce-scatter.2
  575.0 32.2 reduce-scatter.4
Sparse Core Ops, SparseCore 1:
  570.3 250.8 all-reduce.1
where the time goes:
time: 832 us; the launch traced here: 830 us
  blocking collectives  467 us (56%)
  waiting for transfers between devices  280 us (34%)
  matrix products  33.5 us (4%)
  starting transfers between devices  25.7 us (3%)
  between operations  15.9 us (2%)
    psum x3, blocking collectives, balancer_forward_pass(): lax.psum(jnp.sum(expert_density_rows[-1], axis=0), ('dp', 'expert'))  227 us
    psum x3, blocking collectives, balancer_adjoint_pass(): lax.psum(jnp.sum(quotient_grad * division_ratios[repeat], axis=0), ('dp',...  223 us
    psum x1, waiting for transfers between devices, per_device(): grad_router = lax.psum(router_term, ('dp', 'expert'))  206 us
    all_to_all x1, waiting for transfers between devices, per_device(): lax.all_to_all(input_slots.reshape(sources, capacity, model_width), 'expe...  24.8 us
    all_to_all x1, waiting for transfers between devices, per_device(): lax.all_to_all(send_in, 'expert', split_axis=0, concat_axis=0, tiled=True)  23 us
    all_to_all x1, waiting for transfers between devices, per_device(): lax.all_to_all(send_grad, 'expert', split_axis=0, concat_axis=0, tiled=True)  20.2 us
  transfers between devices with their start and end apart: 7, of which 5 were waited for; matrix products, arithmetic and copies ran while one was open for 3% of the time, Pallas kernels for 0%

commit v1 on v0

v1 whole, which is shorter than its diff:
```python
import functools

import jax
import jax.numpy as jnp
from jax import lax
from jax.experimental import pallas as pl
from jax.experimental.pallas import tpu as pltpu
from jax.sharding import PartitionSpec as P

HI = lax.Precision.HIGHEST
F32 = jnp.float32
BF16 = jnp.bfloat16
NE = 32
ND = 8
NX = 4
TOK = 24
CAP = 8
D = 2048
FF = 768
VM = pl.BlockSpec(memory_space=pltpu.VMEM)
MESH = pl.DeviceIdType.MESH


def iota(shape, dim):
    return lax.broadcasted_iota(jnp.int32, shape, dim)


def remote(src, dst, send, recv, dev):
    return pltpu.make_async_remote_copy(
        src_ref=src, dst_ref=dst, send_sem=send, recv_sem=recv, device_id=dev, device_id_type=MESH
    )


def drain(ref, sem):
    pltpu.make_async_copy(ref, ref, sem).wait()


def place():
    me_d = lax.axis_index("dp")
    return me_d, lax.axis_index("expert"), me_d // 2, lax.rem(me_d, 2)


def others(n, body):
    lax.fori_loop(1, n, lambda k, c: (body(k), c)[1], 0)


def greet(me_d, me_e):
    barrier = pltpu.get_barrier_semaphore()
    others(
        NE,
        lambda k: pl.semaphore_signal(
            barrier, inc=1, device_id=(me_d, lax.rem(me_e + k, NE)), device_id_type=MESH
        ),
    )
    others(
        ND,
        lambda k: pl.semaphore_signal(
            barrier, inc=1, device_id=(lax.rem(me_d + k, ND), me_e), device_id_type=MESH
        ),
    )
    pl.semaphore_wait(barrier, NE - 1 + ND - 1)


def own_state(logits, cols):
    lane = iota((TOK, 128), 1)
    d = jnp.where(lane < NE, jnp.exp(logits), 0.0)
    ds, qs = [d], []
    for p in range(3):
        q = d / cols[p : p + 1, :]
        d = q / jnp.sum(q, axis=1, keepdims=True)
        qs.append(q)
        ds.append(d)
    return ds, qs


def dispatch_kernel(
    packed, logits, rank, xs, xr, gate_out, cols, gram,
    lall, dd, gtile, gbuf, s_sem, r_sem, xs_sem, xr_sem, x_s, x_r, p_s, p_r, g_s, g_r,
):
    me_d, me_e, x, core = place()
    greet(me_d, me_e)

    pltpu.make_async_copy(packed, lall.at[core, x, me_e], r_sem).start()
    others(
        NE,
        lambda k: remote(
            packed, lall.at[core, x, me_e], s_sem, r_sem, (me_d, lax.rem(me_e + k, NE))
        ).start(),
    )
    pltpu.make_async_copy(xs.at[me_e], xr.at[me_e], xr_sem).start()

    def send_rows(k):
        to = lax.rem(me_e + k, NE)
        remote(xs.at[to], xr.at[me_e], xs_sem, xr_sem, (me_d, to)).start()

    others(NE, send_rows)

    drain(lall.at[core, x], r_sem)
    others(
        NX,
        lambda k: remote(
            lall.at[core, x], lall.at[core, x], x_s, x_r, (lax.rem(x + k, NX) * 2 + core, me_e)
        ).start(),
    )
    drain(lall.at[core, pl.ds(0, NX - 1)], x_r)
    partner = (x * 2 + 1 - core, me_e)
    pair = remote(lall.at[core], lall.at[core], p_s, p_r, partner)
    pair.start()
    drain(lall.at[1 - core], p_r)

    row = iota((256, 128), 0)
    valid = lax.rem(row, 8) < 6
    li, lj = iota((128, 128), 0), iota((128, 128), 1)
    fold = (lax.rem(li, 32) == lax.rem(lj, 32)).astype(F32)
    block = (li // 32 == lj // 32).astype(F32)

    def rows_of(a):
        return jnp.sum(a.reshape(32, 8, 128), axis=0)

    def first(i, acc):
        d0 = jnp.where(valid, jnp.exp(lall[i // NX, lax.rem(i, NX)].reshape(256, 128)), 0.0)
        dd[i] = d0
        return acc + rows_of(d0)

    acc = lax.fori_loop(0, 8, first, jnp.zeros((8, 128), F32))
    pad = jnp.where(valid, 0.0, 1.0)

    def total(acc):
        one = jnp.broadcast_to(jnp.sum(acc, axis=0, keepdims=True), (8, 128))
        return jnp.dot(one, fold, precision=HI, preferred_element_type=F32)

    c = total(acc)
    cols[0:8, :] = c
    for p in range(2):
        def step(i, carry):
            acc, g = carry
            q = dd[i] / c[0:1, :]
            rs = jnp.dot(q, block, precision=HI, preferred_element_type=F32)
            d = q / (rs + pad)
            dd[i] = d
            g = g + lax.dot_general(
                d, d, (((0,), (0,)), ((), ())), precision=HI, preferred_element_type=F32
            )
            return acc + rows_of(d), g

        acc, g = lax.fori_loop(
            0, 8, step, (jnp.zeros((8, 128), F32), jnp.zeros((128, 128), F32))
        )
        g = jnp.dot(fold, g * block, precision=HI, preferred_element_type=F32)
        gram[p] = jnp.dot(g, fold, precision=HI, preferred_element_type=F32)
        c = total(acc)
        cols[8 * p + 8 : 8 * p + 16, :] = c

    c3 = jnp.concatenate([cols[0:1, :], cols[8:9, :], cols[16:17, :]], axis=0)
    ds, _ = own_state(logits[...], c3)
    gates = NE * ds[3]
    sub = iota((8, 128), 0)
    tile = jnp.zeros((8, 128), F32)
    for slot in range(CAP):
        one = jnp.sum(jnp.where(rank[...] == slot, gates, 0.0), axis=0, keepdims=True)
        tile = tile + jnp.where(sub == slot, jnp.broadcast_to(one, (8, 128)), 0.0)
    gtile[...] = tile
    pltpu.make_async_copy(gtile, gbuf.at[me_e], g_r).start()
    others(
        NE,
        lambda k: remote(
            gtile, gbuf.at[me_e], g_s, g_r, (me_d, lax.rem(me_e + k, NE))
        ).start(),
    )
    drain(gbuf, g_r)
    flat = gbuf[...].reshape(256, 128)
    mine = jnp.sum(jnp.where(iota((256, 128), 1) == me_e, flat, 0.0), axis=1, keepdims=True)
    gate_out[...] = jnp.broadcast_to(mine, (256, 128))

    drain(xr, xr_sem)
    drain(xs.at[pl.ds(0, NE - 1)], xs_sem)
    drain(gbuf.at[pl.ds(0, NE - 1)], g_s)
    drain(lall.at[0, 0, pl.ds(0, NE - 1)], s_sem)
    drain(lall.at[0, pl.ds(0, NX - 1)], x_s)
    pair.wait_send()


def dispatch(packed, logits, rank, xs):
    dma = pltpu.SemaphoreType.DMA
    return pl.pallas_call(
        dispatch_kernel,
        out_shape=(
            jax.ShapeDtypeStruct((NE, 16, D), BF16),
            jax.ShapeDtypeStruct((256, 128), F32),
            jax.ShapeDtypeStruct((24, 128), F32),
            jax.ShapeDtypeStruct((2, 128, 128), F32),
        ),
        in_specs=[VM] * 4,
        out_specs=(VM,) * 4,
        scratch_shapes=[
            pltpu.VMEM((2, NX, NE, 8, 128), F32),
            pltpu.VMEM((8, 256, 128), F32),
            pltpu.VMEM((8, 128), F32),
            pltpu.VMEM((NE, 8, 128), F32),
        ]
        + [dma] * 10,
        compiler_params=pltpu.CompilerParams(collective_id=0, has_side_effects=True),
    )(packed, logits, rank, xs)


def finish_kernel(
    gp, gd, back, score, tokens, logits, rank, cols, gram, rw_t,
    gt_out, pair_out, down_out, router_out,
    rp1, rp2, t1, t2, ra1, ra2, rb1, rb2, u1, u2, w1, w2, rc1, rc2, rd1, rd2,
    ret, sbuf, atile, abuf, btile, bbuf, rsend, rrecv, dsum, drecv, fin,
    p_s, p_r, h_s, h_r, f_s, f_r, ret_s, ret_r, sc_s, sc_r, a_s, a_r, b_s, b_r,
    rs_s, rs_r, d_s, d_r, o_s, o_r,
):
    me_d, me_e, x, core = place()
    greet(me_d, me_e)
    partner = (x * 2 + 1 - core, me_e)
    right = (lax.rem(x + 1, NX) * 2 + core, me_e)
    left = (lax.rem(x + 3, NX) * 2 + core, me_e)

    def plane(src, dst, send, recv):
        pltpu.make_async_copy(src(me_e), dst.at[me_e], recv).start()

        def go(k):
            to = lax.rem(me_e + k, NE)
            remote(src(to), dst.at[me_e], send, recv, (me_d, to)).start()

        others(NE, go)

    plane(lambda e: score.at[e], sbuf, sc_s, sc_r)
    pairs = []
    for n, j in enumerate((2, 1, 3, 0)):
        o = lax.rem(x + j, NX)
        c1 = remote(gp.at[o, 1 - core], rp1.at[j], p_s.at[j, 0], p_r.at[j, 0], partner)
        c2 = remote(gd.at[o, 1 - core], rp2.at[j], p_s.at[j, 1], p_r.at[j, 1], partner)
        c1.start()
        c2.start()
        pairs += [c1, c2]
    plane(lambda e: back.at[e], ret, ret_s, ret_r)

    def got_pair(j):
        drain(rp1.at[j], p_r.at[j, 0])
        drain(rp2.at[j], p_r.at[j, 1])

    def add_rows(n, rows, terms, out):
        def one(i, c):
            at = pl.ds(pl.multiple_of(i * rows, rows), rows)
            out[at, :] = functools.reduce(
                lambda a, b: a + b, [t(at).astype(F32) for t in terms]
            ).astype(BF16)
            return c

        lax.fori_loop(0, n // rows, one, 0)

    def own1(j):
        o = lax.rem(x + j, NX)
        return lambda at: gp[o, core, at, :]

    def own2(j):
        o = lax.rem(x + j, NX)
        return lambda at: gd[o, core, at, :]

    got_pair(2)
    add_rows(256, 32, [own1(2), lambda at: rp1[2, at, :]], t1)
    add_rows(96, 48, [own2(2), lambda at: rp2[2, at, :]], t2)
    half = [
        remote(t1.at[pl.ds(0, 128)], ra1, h_s.at[0], h_r.at[0], right),
        remote(t2.at[pl.ds(0, 48)], ra2, h_s.at[1], h_r.at[1], right),
        remote(t1.at[pl.ds(128, 128)], rb1, h_s.at[2], h_r.at[2], left),
        remote(t2.at[pl.ds(48, 48)], rb2, h_s.at[3], h_r.at[3], left),
    ]
    for c in half:
        c.start()

    c3 = jnp.concatenate([cols[0:1, :], cols[8:9, :], cols[16:17, :]], axis=0)
    ds, qs = own_state(logits[...], c3)
    lane = iota((TOK, 128), 1)
    drain(sbuf, sc_r)
    lane8 = iota((8, 128), 1)
    scores = jnp.zeros((8, 128), F32)
    for e in range(NE):
        scores = scores + jnp.where(lane8 == e, sbuf[e], 0.0)
    grad3 = jnp.zeros((TOK, 128), F32)
    for slot in range(CAP):
        grad3 = grad3 + jnp.where(
            rank[...] == slot, jnp.broadcast_to(scores[slot : slot + 1, :], (TOK, 128)), 0.0
        )
    g = NE * grad3 * ds[3]
    h3 = g - ds[3] * jnp.sum(g, axis=1, keepdims=True)
    atile[...] = jnp.broadcast_to(jnp.sum(h3, axis=0, keepdims=True), (8, 128))
    plane(lambda e: atile, abuf, a_s, a_r)

    got_pair(1)
    got_pair(3)
    for c in half:
        c.wait_recv()

    add_rows(128, 32, [own1(1), lambda at: rp1[1, at, :], lambda at: ra1[at, :]], u1)
    add_rows(48, 48, [own2(1), lambda at: rp2[1, at, :], lambda at: ra2[at, :]], u2)

    def shifted(f, by):
        return lambda at: f(pl.ds(pl.multiple_of(at.start + by, 16), at.size))

    add_rows(
        128, 32, [shifted(own1(1), 128), shifted(lambda at: rp1[1, at, :], 128)],
        u1.at[pl.ds(128, 128)],
    )
    add_rows(
        48, 48, [shifted(own2(1), 48), shifted(lambda at: rp2[1, at, :], 48)],
        u2.at[pl.ds(48, 48)],
    )
    full = [
        remote(u1, rc1, f_s.at[0], f_r.at[0], right),
        remote(u2, rc2, f_s.at[1], f_r.at[1], right),
    ]
    full[0].start()
    full[1].start()
    add_rows(128, 32, [own1(3), lambda at: rp1[3, at, :]], w1)
    add_rows(48, 48, [own2(3), lambda at: rp2[3, at, :]], w2)
    add_rows(
        128, 32,
        [shifted(own1(3), 128), shifted(lambda at: rp1[3, at, :], 128), lambda at: rb1[at, :]],
        w1.at[pl.ds(128, 128)],
    )
    add_rows(
        48, 48,
        [shifted(own2(3), 48), shifted(lambda at: rp2[3, at, :], 48), lambda at: rb2[at, :]],
        w2.at[pl.ds(48, 48)],
    )
    full += [
        remote(w1, rd1, f_s.at[2], f_r.at[2], left),
        remote(w2, rd2, f_s.at[3], f_r.at[3], left),
    ]
    full[2].start()
    full[3].start()

    drain(abuf, a_r)
    btile[...] = jnp.sum(abuf[...], axis=0)
    pltpu.make_async_copy(btile, bbuf.at[me_d], b_r).start()
    others(
        ND,
        lambda k: remote(
            btile, bbuf.at[me_d], b_s, b_r, (lax.rem(me_d + k, ND), me_e)
        ).start(),
    )
    gates = NE * ds[3]
    ex_i, ex_j = iota((128, 512), 0), iota((128, 512), 1)
    spread = ((ex_i < NE) & (ex_j // 16 == ex_i)).astype(BF16)
    g_hi = gates.astype(BF16)
    g_lo = (gates - g_hi.astype(F32)).astype(BF16)
    wide = jnp.dot(
        jnp.concatenate([rank[...], g_hi.astype(F32), g_lo.astype(F32)], axis=0).astype(BF16),
        spread,
        preferred_element_type=F32,
    )
    k16 = lax.rem(iota((TOK, 512), 1), 16)
    rank_w = wide[0:TOK].astype(jnp.int32)
    left_m, right_m = rank_w == k16, rank_w == k16 - 8
    parts = []
    for m in (left_m, right_m):
        parts += [jnp.where(m, wide[TOK : 2 * TOK], 0.0), jnp.where(m, wide[2 * TOK :], 0.0)]
    weights = jnp.concatenate(parts, axis=0).astype(BF16)

    drain(bbuf, b_r)
    v = jnp.sum(bbuf[...], axis=0)
    first32 = lane8 < NE
    u = jnp.dot(
        jnp.where(first32, v / cols[16:24, :], 0.0), gram[1], precision=HI,
        preferred_element_type=F32,
    )
    s = jnp.dot(
        jnp.where(first32, u / cols[8:16, :], 0.0), gram[0], precision=HI,
        preferred_element_type=F32,
    )
    qv = qs[2] * v[0:1, :]
    h2 = h3 - qv + ds[2] * jnp.sum(qv, axis=1, keepdims=True)
    qu = qs[1] * u[0:1, :]
    h1 = h2 - qu + ds[1] * jnp.sum(qu, axis=1, keepdims=True)
    lgrad = (h1 - qs[0] * s[0:1, :]).astype(BF16)[:, :NE]
    router_t = lax.dot_general(
        lgrad, tokens[...], (((0,), (0,)), ((), ())), preferred_element_type=F32
    )
    for p in range(NE):
        h, b = p % 2, p // 2
        rsend[p] = router_t[16 * h : 16 * h + 16, 128 * b : 128 * b + 128]
    plane(lambda e: rsend.at[e], rrecv, rs_s, rs_r)
    router_in = jnp.dot(lgrad, rw_t[...], preferred_element_type=F32)

    drain(ret, ret_r)
    flat = ret[...].reshape(512, 1024)
    mixed = jnp.dot(weights, flat, preferred_element_type=F32)
    gt_out[:, 0:1024] = (mixed[0:24] + mixed[24:48] + router_in[:, 0:1024]).astype(BF16)
    gt_out[:, 1024:2048] = (mixed[48:72] + mixed[72:96] + router_in[:, 1024:2048]).astype(BF16)

    drain(rrecv, rs_r)
    dsum[...] = jnp.sum(rrecv[...], axis=0)
    pltpu.make_async_copy(dsum, drecv.at[me_d], d_r).start()
    others(
        ND,
        lambda k: remote(
            dsum, drecv.at[me_d], d_s, d_r, (lax.rem(me_d + k, ND), me_e)
        ).start(),
    )
    drain(drecv, d_r)
    fin[...] = jnp.sum(drecv[...], axis=0)
    plane(lambda e: fin, router_out, o_s, o_r)

    got_pair(0)
    for c in full:
        c.wait_recv()
    add_rows(
        256, 32,
        [own1(0), lambda at: rp1[0, at, :], lambda at: rc1[at, :], lambda at: rd1[at, :]],
        pair_out,
    )
    add_rows(
        96, 48,
        [own2(0), lambda at: rp2[0, at, :], lambda at: rc2[at, :], lambda at: rd2[at, :]],
        down_out,
    )
    drain(router_out, o_r)
    for c in pairs + half + full:
        c.wait_send()
    drain(ret.at[pl.ds(0, NE - 1)], ret_s)
    drain(sbuf.at[pl.ds(0, NE - 1)], sc_s)
    drain(abuf.at[pl.ds(0, NE - 1)], a_s)
    drain(bbuf.at[pl.ds(0, ND - 1)], b_s)
    drain(rrecv.at[pl.ds(0, NE - 1)], rs_s)
    drain(drecv.at[pl.ds(0, ND - 1)], d_s)
    drain(router_out.at[pl.ds(0, NE - 1)], o_s)


def finish(*args):
    dma = pltpu.SemaphoreType.DMA
    V = pltpu.VMEM
    return pl.pallas_call(
        finish_kernel,
        out_shape=(
            jax.ShapeDtypeStruct((TOK, D), BF16),
            jax.ShapeDtypeStruct((256, 2 * FF), BF16),
            jax.ShapeDtypeStruct((96, D), BF16),
            jax.ShapeDtypeStruct((NE, 16, 128), F32),
        ),
        in_specs=[VM] * 10,
        out_specs=(VM,) * 4,
        scratch_shapes=[
            V((4, 256, 2 * FF), BF16), V((4, 96, D), BF16),
            V((256, 2 * FF), BF16), V((96, D), BF16),
            V((128, 2 * FF), BF16), V((48, D), BF16),
            V((128, 2 * FF), BF16), V((48, D), BF16),
            V((256, 2 * FF), BF16), V((96, D), BF16),
            V((256, 2 * FF), BF16), V((96, D), BF16),
            V((256, 2 * FF), BF16), V((96, D), BF16),
            V((256, 2 * FF), BF16), V((96, D), BF16),
            V((NE, 16, 1024), BF16),
            V((NE, 8, 128), F32),
            V((8, 128), F32), V((NE, 8, 128), F32),
            V((8, 128), F32), V((ND, 8, 128), F32),
            V((NE, 16, 128), F32), V((NE, 16, 128), F32),
            V((16, 128), F32), V((ND, 16, 128), F32), V((16, 128), F32),
            dma((4, 2)), dma((4, 2)), dma((4,)), dma((4,)), dma((4,)), dma((4,)),
        ]
        + [dma] * 14,
        compiler_params=pltpu.CompilerParams(
            collective_id=1, has_side_effects=True, vmem_limit_bytes=60 * 1024 * 1024
        ),
    )(*args)


def column_product(a, b):
    return lax.dot_general(a, b, (((0,), (0,)), ((), ())), preferred_element_type=F32)


def per_device(tokens, out_grad, expert_ids, router_weight, w_gate, w_up, w_down):
    wg, wu, wd = w_gate[0], w_up[0], w_down[0]
    logits = jnp.dot(tokens, router_weight, preferred_element_type=F32)
    er = jnp.arange(NE, dtype=jnp.int32)
    picked = jnp.sum((expert_ids[:, :, None] == er).astype(jnp.int32), axis=1)
    before = (jnp.arange(TOK)[:, None] > jnp.arange(TOK)[None, :]).astype(BF16)
    rank = jnp.dot(before, picked.astype(BF16), preferred_element_type=F32).astype(jnp.int32)
    rank = jnp.where(picked > 0, rank, -64)
    packed = jnp.pad(logits.reshape(6, 128), ((0, 2), (0, 0)))
    logits_w = jnp.pad(logits, ((0, 0), (0, 96)))
    rank_w = jnp.pad(rank, ((0, 0), (0, 96)), constant_values=-64)
    sel = (rank.T[:, None, :] == jnp.arange(CAP)[None, :, None]).astype(BF16)
    zero = jnp.zeros_like(sel)
    both = jnp.concatenate(
        [jnp.concatenate([sel, zero], axis=2), jnp.concatenate([zero, sel], axis=2)], axis=1
    )
    xs = jnp.einsum(
        "ekt,td->ekd", both, jnp.concatenate([tokens, out_grad], axis=0),
        preferred_element_type=F32,
    ).astype(BF16)
    xr, gate_b, cols, gram = dispatch(packed, logits_w, rank_w, xs)

    flat_in = xr[:, :CAP].reshape(256, D)
    flat_grad = xr[:, CAP:].reshape(256, D)
    gate = gate_b[:, 0:1].astype(BF16).astype(F32)
    gate_pre = jnp.dot(flat_in, wg, preferred_element_type=F32)
    up_pre = jnp.dot(flat_in, wu, preferred_element_type=F32)
    sg = jax.nn.sigmoid(gate_pre)
    act = gate_pre * sg
    hidden = act * up_pre
    tc = (((1,), (1,)), ((), ()))
    hgrad = lax.dot_general(flat_grad, wd, tc, preferred_element_type=F32)
    score = jnp.sum(hgrad * hidden, axis=1, keepdims=True).astype(BF16).astype(F32)
    ggrad = (hgrad * up_pre * sg * (1.0 + gate_pre * (1.0 - sg))).astype(BF16)
    ugrad = (hgrad * act).astype(BF16)
    igrad = lax.dot_general(ggrad, wg, tc, preferred_element_type=F32)
    igrad = igrad + lax.dot_general(ugrad, wu, tc, preferred_element_type=F32)
    back = igrad.astype(BF16).reshape(NE, CAP, 2, 1024).transpose(0, 2, 1, 3).reshape(NE, 16, 1024)
    paired = jnp.concatenate([(gate * ggrad).astype(BF16), (gate * ugrad).astype(BF16)], axis=1)
    gp = column_product(flat_in, paired).astype(BF16).reshape(NX, 2, 256, 2 * FF)
    gd = column_product(hidden.astype(BF16), (gate * flat_grad).astype(BF16)).astype(BF16)
    gd = gd.reshape(NX, 2, 96, D)
    score_b = jnp.broadcast_to(score, (256, 128)).reshape(NE, CAP, 128)
    gt, pair, down, router = finish(
        gp, gd, back, score_b, tokens, logits_w, rank_w, cols, gram, router_weight.T
    )
    grad_router = router.reshape(16, 2, 16, 128).transpose(0, 3, 1, 2).reshape(D, NE)
    return gt, grad_router, pair[None, :, :FF], pair[None, :, FF:], down[None]


def solution(mesh):
    in_specs = (
        P(("dp", "expert"), None), P(("dp", "expert"), None), P(("dp", "expert"), None), P(),
        P("expert", None, None), P("expert", None, None), P("expert", None, None),
    )
    out_specs = (
        P(("dp", "expert"), None), P(),
        P("expert", "dp", None), P("expert", "dp", None), P("expert", "dp", None),
    )
    return jax.shard_map(
        per_device, mesh=mesh, in_specs=in_specs, out_specs=out_specs, check_vma=False
    )
```

time: 832 us -> 182 us (0.22)
  blocking collectives: 467 us -> 0 us
  waiting for transfers between devices: 280 us -> 0 us
  Pallas kernels: 0 us -> 148 us
  starting transfers between devices: 25.7 us -> 0 us
  between operations: 15.9 us -> 0.76 us
  matrix products: 33.5 us -> 20.5 us
    psum x6 -> x0, blocking collectives: 450 us -> none  [the longest x3 227 us: balancer_forward_pass(): lax.psum(jnp.sum(expert_density_rows[-1], axis=0), ('dp', 'expert'))]
    psum x1 -> x0, waiting for transfers between devices: 206 us -> none  [per_device(): grad_router = lax.psum(router_term, ('dp', 'expert'))]
    pallas_call x0 -> x2, Pallas kernels: none -> 148 us  [the longest x1 81.4 us: finish(): pl.pallas_call(finish_kernel, out_shape=(jax.ShapeDtypeStruct((TOK, D), B...]
    all_to_all x4 -> x0, waiting for transfers between devices: 74.1 us -> none  [the longest x1 24.8 us: per_device(): lax.all_to_all(input_slots.reshape(sources, capacity, model_width), 'expe...]
    all_to_all x4 -> x0, starting transfers between devices: 25.6 us -> none  [the longest x1 8.27 us: per_device(): lax.all_to_all(send_grad, 'expert', split_axis=0, concat_axis=0, tiled=True)]
    all_to_all x1 -> x0, blocking collectives: 16.5 us -> none  [per_device(): lax.all_to_all(score_slots.reshape(sources, capacity), 'expert', split_ax...]
    dot_general x13 -> x10, matrix products: 33.5 us -> 20.5 us  [the longest x2 7.39 us: column_product(): lax.dot_general(a, b, (((0,), (0,)), ((), ())), preferred_element_type=F32)]
  transfers between devices with their start and end apart: 7 -> 0, of which waited for: 5 -> 0; matrix products, arithmetic and copies ran while one was open for 3% -> 0% of each run, Pallas kernels for 0% -> 0%
where the time goes in v1:
time: 182 us; the launch traced here: 181 us
  Pallas kernels  148 us (81%)
  matrix products  20.5 us (11%)
  local copies, waits for them, and re-layouts  12.3 us (7%)
    pallas_call x1, Pallas kernels, finish(): pl.pallas_call(finish_kernel, out_shape=(jax.ShapeDtypeStruct((TOK, D), B...  81.4 us
    pallas_call x1, Pallas kernels, dispatch(): pl.pallas_call(dispatch_kernel, out_shape=(jax.ShapeDtypeStruct((NE, 16,...  66.3 us
    dot_general x2, matrix products, column_product(): lax.dot_general(a, b, (((0,), (0,)), ((), ())), preferred_element_type=F32)  7.39 us
    unnamed x14, local copies, waits for them, and re-layouts  6.31 us

profile of v1, /device:TPU:1, one launch (start us, length us, event | category | flops | bytes accessed | tf_op | source)
XLA Modules:
  0.0 181.4 jit_solution(14105666635677445988)
XLA Ops:
  0.6 0.0 copy-start
  0.6 0.9 copy.18
  1.6 0.1 convert_reduce_fusion.1
  1.7 0.1 fusion.16
  1.8 0.6 pad.16.rank
  2.4 1.1 fusion.52
  3.5 0.6 pad.15.logits
  4.1 0.1 copy.19
  4.2 3.0 %convolution_convert_fusion.2.xs = bf16[32,16,2048]{2,1,0:T(8,128)(2,1)} fusion(bf16[24,2048]{1,0:T(8,128)(2,1)} %param.8, bf16[24,2048]{1,0:T(8,128)(2,1)} %tokens.1, bf16[32,8,24]{2,1,0:T(8,128)(2,1)S(1)} %fusion.44), kind=kOutput, calls=%fused_computation.12 | convolution fusion | flops 102301696 | bytes 2306048 | tf_op jit(solution)/shard_map/ekt,td->ekd/dot_general | solution.py:489
  7.3 0.1 reshape.55
  7.3 0.6 pad.14.packed
  7.9 66.3 %shard_map.110 = (bf16[32,16,2048]{2,1,0:T(8,128)(2,1)}, f32[256,128]{1,0:T(8,128)}, f32[24,128]{1,0:T(8,128)}, f32[2,128,128]{2,1,0:T(8,128)}) custom-call(f32[8,128]{1,0:T(8,128)} %pad.14.packed, f32[24,128]{1,0:T(8,128)} %pad.15.logits, s32[24,128]{1,0:T(8,128)} %pad.16.rank, bf16[32,16,2048]{2,1,0:T(8,128)(2,1)} %convolution_convert_fusion.2.xs), custom_call_target="tpu_custom_call" | custom-call | tf_op jit(solution)/shard_map/pallas_call | solution.py:185
  74.2 0.0 copy-start.2
  74.2 0.0 copy-start.4
  74.2 3.3 %fusion.6 = f32[256,768]{1,0:T(8,128)S(1)} fusion(bf16[1,2048,768]{2,1,0:T(8,128)(2,1)} %param.12, bf16[32,16,2048]{2,1,0:T(8,128)(2,1)} %get-tuple-element.13), kind=kOutput, calls=%fused_computation.8 | convolution fusion | flops 805306368 | bytes 4980736 | tf_op jit(solution)/shard_map/dot_general | solution.py:499
  77.6 0.0 copy-done.2
  77.6 0.4 copy-done.4
  78.0 0.0 copy-start.3
  78.0 1.0 fusion.8
  79.0 0.0 copy-done.3
  79.1 0.1 convert_reduce_fusion
  79.2 0.0 copy-done
  79.2 1.5 multiply_convert_fusion.4
  80.7 0.0 copy-start.1
  80.7 1.0 fusion
  81.7 0.9 copy-done.1
  82.6 2.0 %fusion.13 = bf16[256,2048]{1,0:T(8,128)(2,1)} fusion(f32[256,2048]{1,0:T(8,128)S(1)} %fusion, bf16[256,768]{1,0:T(8,128)(2,1)S(1)} %get-tuple-element.27, bf16[1,2048,768]{2,1,0:T(8,128)(2,1)S(1)} %copy-done.1), kind=kOutput, calls=%fused_computation.14 | convolution fusion | flops 806354944 | bytes 6684672 | tf_op jit(solution)/shard_map/dot_general | solution.py:509
  84.6 2.9 %convolution_convert_fusion.1 = bf16[768,2048]{1,0:T(8,128)(2,1)} fusion(f32[256]{0:T(256)S(1)} %convert_reduce_fusion, bf16[32,16,2048]{2,1,0:T(8,128)(2,1)S(1)} %copy-done.2, f32[256,768]{1,0:T(8,128)S(1)} %fusion.6, f32[256,768]{1,0:T(8,128)S(1)} %get-tuple-element.30), kind=kOutput, calls=%fused_computation.1 | convolution fusion | flops 809631744 | bytes 5768192 | tf_op jit(solution)/shard_map/dot_general | solution.py:470
  87.5 4.5 %convolution_convert_fusion = bf16[2048,1536]{1,0:T(8,128)(2,1)} fusion(bf16[32,16,2048]{2,1,0:T(8,128)(2,1)S(1)} %copy-done.2, bf16[256,768]{1,0:T(8,128)(2,1)S(1)} %get-tuple-element.26, bf16[256,768]{1,0:T(8,128)(2,1)S(1)} %get-tuple-element.21), kind=kOutput, calls=%fused_computation | convolution fusion | flops 1615331328 | bytes 8126464 | tf_op jit(solution)/shard_map/dot_general | solution.py:470
  91.9 0.1 reshape.65
  92.0 0.8 broadcast_in_dim.13.score
  92.8 81.4 %shard_map.111 = (bf16[24,2048]{1,0:T(8,128)(2,1)}, bf16[256,1536]{1,0:T(8,128)(2,1)}, bf16[96,2048]{1,0:T(8,128)(2,1)}, f32[32,16,128]{2,1,0:T(8,128)}) custom-call(bf16[4,2,256,1536]{3,2,1,0:T(8,128)(2,1)} %bitcast.66, bf16[4,2,96,2048]{3,2,1,0:T(8,128)(2,1)} %bitcast.68, bf16[32,16,1024]{2,1,0:T(8,128)(2,1)} %bitcast.67, ...), custom_call_target="tpu_custom_call" | custom-call | tf_op jit(solution)/shard_map/pallas_call | solution.py:435
  174.2 2.0 %slice_bitcast_fusion = (bf16[1,256,768]{2,1,0:T(8,128)(2,1)}, bf16[1,256,768]{2,1,0:T(8,128)(2,1)}) fusion(bf16[256,1536]{1,0:T(8,128)(2,1)} %get-tuple-element.19), kind=kLoop, calls=%fused_computation.39 | loop fusion | bytes 1572864 | tf_op jit(solution)/shard_map/broadcast_in_dim | solution.py:520
  176.2 1.1 copy.20
  177.3 0.8 copy.23
  178.1 1.5 copy.26
  179.6 1.8 copy.27
  (1 shorter events, 0.0 us)
Async XLA Ops:
  0.6 78.5 %copy-start = (bf16[1,2048,768]{2,1,0:T(8,128)(2,1)S(1)}, bf16[1,2048,768]{2,1,0:T(8,128)(2,1)}, u32[]{:S(2)}) copy-start(bf16[1,2048,768]{2,1,0:T(8,128)(2,1)} %param.11) | copy-start | bytes 9437188
  74.2 3.4 %copy-start.2 = (bf16[32,16,2048]{2,1,0:T(8,128)(2,1)S(1)}, bf16[32,16,2048]{2,1,0:T(8,128)(2,1)}, u32[]{:S(2)}) copy-start(bf16[32,16,2048]{2,1,0:T(8,128)(2,1)} %get-tuple-element.13) | copy-start | bytes 6291460
  74.2 3.8 %copy-start.4 = (bf16[1,768,2048]{2,1,0:T(8,128)(2,1)S(1)}, bf16[1,768,2048]{2,1,0:T(8,128)(2,1)}, u32[]{:S(2)}) copy-start(bf16[1,768,2048]{2,1,0:T(8,128)(2,1)} %param.13) | copy-start | bytes 9437188
  78.0 1.0 copy-start.3
  80.7 1.9 %copy-start.1 = (bf16[1,2048,768]{2,1,0:T(8,128)(2,1)S(1)}, bf16[1,2048,768]{2,1,0:T(8,128)(2,1)}, u32[]{:S(2)}) copy-start(bf16[1,2048,768]{2,1,0:T(8,128)(2,1)} %param.12) | copy-start | bytes 9437188

commit v2 on v1

v2 whole, which is shorter than its diff:
```python
import functools

import jax
import jax.numpy as jnp
from jax import lax
from jax.experimental import pallas as pl
from jax.experimental.pallas import tpu as pltpu
from jax.sharding import PartitionSpec as P

HI = lax.Precision.HIGHEST
F32 = jnp.float32
BF16 = jnp.bfloat16
NE = 32
ND = 8
NX = 4
TOK = 24
CAP = 8
D = 2048
FF = 768
VM = pl.BlockSpec(memory_space=pltpu.VMEM)
MESH = pl.DeviceIdType.MESH


def iota(shape, dim):
    return lax.broadcasted_iota(jnp.int32, shape, dim)


def remote(src, dst, send, recv, dev):
    return pltpu.make_async_remote_copy(
        src_ref=src, dst_ref=dst, send_sem=send, recv_sem=recv, device_id=dev, device_id_type=MESH
    )


def drain(ref, sem):
    pltpu.make_async_copy(ref, ref, sem).wait()


def place():
    me_d = lax.axis_index("dp")
    return me_d, lax.axis_index("expert"), me_d // 2, lax.rem(me_d, 2)


def others(n, body):
    lax.fori_loop(1, n, lambda k, c: (body(k), c)[1], 0)


def greet(me_d, me_e):
    barrier = pltpu.get_barrier_semaphore()
    others(
        NE,
        lambda k: pl.semaphore_signal(
            barrier, inc=1, device_id=(me_d, lax.rem(me_e + k, NE)), device_id_type=MESH
        ),
    )
    others(
        ND,
        lambda k: pl.semaphore_signal(
            barrier, inc=1, device_id=(lax.rem(me_d + k, ND), me_e), device_id_type=MESH
        ),
    )
    pl.semaphore_wait(barrier, NE - 1 + ND - 1)


def own_state(logits, cols):
    lane = iota((TOK, 128), 1)
    d = jnp.where(lane < NE, jnp.exp(logits), 0.0)
    ds, qs = [d], []
    for p in range(3):
        q = d / cols[p : p + 1, :]
        d = q / jnp.sum(q, axis=1, keepdims=True)
        qs.append(q)
        ds.append(d)
    return ds, qs


NT = (((1,), (1,)), ((), ()))
TN = (((0,), (0,)), ((), ()))


def mm(a, b, dims=None, exact=False):
    dims = dims or (((1,), (0,)), ((), ()))
    return lax.dot_general(
        a, b, dims, precision=HI if exact else None, preferred_element_type=F32
    )


def moe_kernel(
    tokens, grads, ids, rw, wg_hbm, wu_hbm, wd_hbm,
    gt_out, pair_out, down_out, router_out,
    wg, wu, wd, packed, rk, rkbuf, lall, dd, cols, gram, gtile, gbuf,
    zt, zg, yt, yg, rt, rg, pt, hid, act, dsl, ht, pht, ds, pds, gg, ug, pair, ppair,
    g1, g2, ra1, ra2, rb1, rb2, rc1, rc2, rd1, rd2,
    bsend, ret, stile, sbuf, atile, abuf, btile, bbuf, rsend, rrecv, dsum, drecv, fin,
    w_sem, zs_t, zr_t, zs_g, zr_g, ys_t, yr_t, ys_g, yr_g, q_s, q_r, h_s, h_r, n_s, n_r, m_s, m_r,
    lg_s, lg_r, rk_s, rk_r, x_s, x_r, p_s, p_r, g_s, g_r, ret_s, ret_r, sc_s, sc_r,
    a_s, a_r, b_s, b_r, rs_s, rs_r, d_s, d_r, o_s, o_r,
):
    me_d, me_e, x, core = place()
    y, z = me_e // 8, lax.rem(me_e, 8)
    barrier = pltpu.get_barrier_semaphore()
    others(
        NE,
        lambda k: pl.semaphore_signal(
            barrier, inc=1, device_id=(me_d, lax.rem(me_e + k, NE)), device_id_type=MESH
        ),
    )
    others(
        ND,
        lambda k: pl.semaphore_signal(
            barrier, inc=1, device_id=(lax.rem(me_d + k, ND), me_e), device_id_type=MESH
        ),
    )
    loads = [
        pltpu.make_async_copy(a.at[0], b, w_sem.at[n])
        for n, (a, b) in enumerate(((wg_hbm, wg), (wu_hbm, wu), (wd_hbm, wd)))
    ]
    for c in loads:
        c.start()
    partner = (x * 2 + 1 - core, me_e)
    right = (lax.rem(x + 1, NX) * 2 + core, me_e)
    left = (lax.rem(x + 3, NX) * 2 + core, me_e)
    z_up = (me_d, y * 8 + lax.rem(z + 1, 8))
    z_down = (me_d, y * 8 + lax.rem(z + 7, 8))

    lane24 = iota((TOK, 128), 1)
    lane8, sub8 = iota((8, 128), 1), iota((8, 128), 0)
    logits = jnp.concatenate(
        [mm(tokens[...], rw[...]), jnp.zeros((TOK, 96), F32)], axis=1
    )
    packed[...] = (
        logits[0:8] + pltpu.roll(logits[8:16], 32, 1) + pltpu.roll(logits[16:24], 64, 1)
    )
    picked = jnp.zeros((TOK, 128), F32)
    for k in range(8):
        picked = picked + (ids[:, k : k + 1] == lane24).astype(F32)
    before = (iota((TOK, TOK), 0) > iota((TOK, TOK), 1)).astype(BF16)
    rank = jnp.where(picked > 0, mm(before, picked.astype(BF16)), -64.0)
    rank_pad = jnp.concatenate([rank, jnp.full((104, 128), -64.0, F32)], axis=0).astype(BF16)
    pi, pj = iota((64, 128), 0), iota((64, 128), 1)
    place_rows = ((lax.rem(pi, 8) < 4) & (pj == lax.rem(pi, 8) * 8 + pi // 8)).astype(BF16)
    rk[...] = mm(place_rows, rank_pad, NT).reshape(8, 8, 128)

    pl.semaphore_wait(barrier, NE - 1 + ND - 1)

    def z_ring(k):
        to = lax.rem(z + k, 8)
        remote(rk.at[to], rkbuf.at[z], rk_s, rk_r, (me_d, y * 8 + to)).start()

    pltpu.make_async_copy(rk.at[z], rkbuf.at[z], rk_r).start()
    others(8, z_ring)

    def z_copy(own, buf, ss, rs, k, sign):
        at = lambda n: (8 + sign * n) % 8
        return remote(
            own if k == 1 else buf.at[at(k - 1)], buf.at[at(k)], ss.at[at(k)], rs.at[at(k)],
            z_down if sign > 0 else z_up,
        )

    t_dn = [z_copy(tokens, zt, zs_t, zr_t, k, -1) for k in (1, 2, 3, 4)]
    t_up = [z_copy(tokens, zt, zs_t, zr_t, k, 1) for k in (1, 2, 3)]
    g_dn = [z_copy(grads, zg, zs_g, zr_g, k, -1) for k in (1, 2, 3)]
    g_up = [z_copy(grads, zg, zs_g, zr_g, k, 1) for k in (1, 2, 3, 4)]
    t_dn[0].start()
    t_up[0].start()

    def plane(src, dst, send, recv):
        pltpu.make_async_copy(src(me_e), dst, recv).start()

        def go(k):
            to = lax.rem(me_e + k, NE)
            remote(src(to), dst, send, recv, (me_d, to)).start()

        others(NE, go)

    plane(lambda e: packed, lall.at[core, x, me_e], lg_s, lg_r)
    g_dn[0].start()
    g_up[0].start()

    drain(rkbuf, rk_r)

    def choose(zs, half):
        parts = []
        for yy in range(4):
            row = rkbuf[zs, yy : yy + 1, :]
            hot = (jnp.broadcast_to(row, (8, 128)) == sub8.astype(F32)).astype(F32)
            none = jnp.zeros((8, 128), F32)
            parts += [hot, none] if half == 0 else [none, hot]
        return jnp.concatenate(parts, axis=0).astype(BF16)[:, :TOK]

    y_copies = []

    def y_phase(j, own, buf, send_buf, recv_buf, ss, rs):
        first = own[...] if j == 0 else buf[j]
        out = mm(choose(lax.rem(z + j, 8), 0), first)
        out = out + mm(choose(lax.rem(z + 7 - j, 8), 1), buf[7 - j])
        send_buf[j] = out.astype(BF16).reshape(4, 16, D)
        for m in range(1, 4):
            to = lax.rem(y + m, 4)
            c = remote(
                send_buf.at[j, to], recv_buf.at[y, j], ss.at[j, m], rs.at[j, m],
                (me_d, to * 8 + z),
            )
            c.start()
            y_copies.append(c)
        c = pltpu.make_async_copy(send_buf.at[j, y], recv_buf.at[y, j], rs.at[j, 0])
        c.start()

    def y_wait(recv_buf, rs):
        for j in range(4):
            for m in range(4):
                drain(recv_buf.at[0, 0], rs.at[j, m])

    t_dn[0].wait_recv()
    t_dn[1].start()
    t_up[0].wait_recv()
    t_up[1].start()
    y_phase(0, tokens, zt, yt, rt, ys_t, yr_t)
    g_dn[0].wait_recv()
    g_dn[1].start()
    g_up[0].wait_recv()
    g_up[1].start()
    t_dn[1].wait_recv()
    t_dn[2].start()
    t_up[1].wait_recv()
    t_up[2].start()
    y_phase(1, tokens, zt, yt, rt, ys_t, yr_t)

    drain(lall.at[core, x], lg_r)
    others(
        NX,
        lambda k: remote(
            lall.at[core, x], lall.at[core, x], x_s, x_r, (lax.rem(x + k, NX) * 2 + core, me_e)
        ).start(),
    )

    g_dn[1].wait_recv()
    g_dn[2].start()
    g_up[1].wait_recv()
    g_up[2].start()
    t_dn[2].wait_recv()
    t_dn[3].start()
    t_up[2].wait_recv()
    y_phase(2, tokens, zt, yt, rt, ys_t, yr_t)
    y_phase(0, grads, zg, yg, rg, ys_g, yr_g)
    g_dn[2].wait_recv()
    g_up[2].wait_recv()
    g_up[3].start()
    t_dn[3].wait_recv()
    y_phase(3, tokens, zt, yt, rt, ys_t, yr_t)
    y_phase(1, grads, zg, yg, rg, ys_g, yr_g)
    y_phase(2, grads, zg, yg, rg, ys_g, yr_g)
    drain(lall.at[core, pl.ds(0, NX - 1)], x_r)
    logit_pair = remote(lall.at[core], lall.at[core], p_s, p_r, partner)
    logit_pair.start()
    g_up[3].wait_recv()
    y_phase(3, grads, zg, yg, rg, ys_g, yr_g)
    drain(lall.at[1 - core], p_r)

    valid = iota((256, 128), 1) < 96
    li, lj = iota((128, 128), 0), iota((128, 128), 1)
    fold = (lax.rem(li, 32) == lax.rem(lj, 32)).astype(F32)
    block = (li // 32 == lj // 32).astype(F32)

    def rows_of(a):
        return jnp.sum(a.reshape(32, 8, 128), axis=0)

    def first(i, acc):
        d0 = jnp.where(valid, jnp.exp(lall[i // NX, lax.rem(i, NX)].reshape(256, 128)), 0.0)
        dd[i] = d0
        return acc + rows_of(d0)

    acc = lax.fori_loop(0, 8, first, jnp.zeros((8, 128), F32))
    pad = jnp.where(valid, 0.0, 1.0)

    def total(acc):
        one = jnp.broadcast_to(jnp.sum(acc, axis=0, keepdims=True), (8, 128))
        return mm(one, fold, exact=True)

    c = total(acc)
    cols[0:8, :] = c
    for p in range(2):
        def step(i, carry):
            acc, g = carry
            q = dd[i] / c[0:1, :]
            d = q / (mm(q, block, exact=True) + pad)
            dd[i] = d
            return acc + rows_of(d), g + mm(d, d, TN, exact=True)

        acc, g = lax.fori_loop(
            0, 8, step, (jnp.zeros((8, 128), F32), jnp.zeros((128, 128), F32))
        )
        gram[p] = mm(mm(fold, g * block, exact=True), fold, exact=True)
        c = total(acc)
        cols[8 * p + 8 : 8 * p + 16, :] = c

    c3 = jnp.concatenate([cols[0:1, :], cols[8:9, :], cols[16:17, :]], axis=0)
    dens, quot = own_state(logits, c3)
    gates = NE * dens[3]
    tile = jnp.zeros((8, 128), F32)
    for slot in range(CAP):
        one = jnp.sum(jnp.where(rank == slot, gates, 0.0), axis=0, keepdims=True)
        tile = tile + jnp.where(sub8 == slot, jnp.broadcast_to(one, (8, 128)), 0.0)
    gtile[...] = tile
    plane(lambda e: gtile, gbuf.at[me_e], g_s, g_r)

    for c in loads:
        c.wait()
    y_wait(rt, yr_t)
    cuts = []
    for o in range(4):
        at = pl.ds(pl.multiple_of(512 * o + 256 * (1 - core), 256), 256)
        cuts.append(
            remote(rt.at[:, :, :, at], pt.at[o], q_s.at[o], q_r.at[o], partner)
        )
        cuts[-1].start()

    def forward(i, carry):
        at = pl.ds(pl.multiple_of(i * 256, 256), 256)
        rows = rt[...].reshape(256, D)
        gate_pre = mm(rows, wg[:, at])
        up_pre = mm(rows, wu[:, at])
        sg = jax.nn.sigmoid(gate_pre)
        a = gate_pre * sg
        h = a * up_pre
        hid[:, at] = h
        act[:, at] = a
        dsl[:, at] = up_pre * sg * (1.0 + gate_pre * (1.0 - sg))
        ht[at, :] = h.T.astype(BF16)
        return carry

    lax.fori_loop(0, 3, forward, 0)
    ht_copy = remote(ht, pht, q_s.at[4], q_r.at[4], partner)
    ht_copy.start()

    def where_from(k):
        o = lax.rem(k, 8)
        j, h = o // 2, lax.rem(o, 2)
        yy = lax.rem(y + k // 8, 4)
        zz = lax.rem(z + j - h * (2 * j + 1) + 16, 8)
        return yy * 8 + o, yy * 8 + zz

    drain(gbuf, g_r)
    tiles = []
    for yy in range(4):
        for o in range(8):
            j, h = o // 2, o % 2
            tiles.append(gbuf[yy * 8 + lax.rem(z + (j if h == 0 else 7 - j), 8)])
    gate = jnp.sum(
        jnp.where(iota((256, 128), 1) == me_e, jnp.concatenate(tiles, axis=0), 0.0),
        axis=1, keepdims=True,
    ).astype(BF16).astype(F32)

    y_wait(rg, yr_g)
    for b in range(4):
        at = slice(512 * b, 512 * b + 512)
        ds[:, at] = (gate * rg[:, :, :, at].reshape(256, 512).astype(F32)).astype(BF16)
    ds_copy = remote(ds, pds, q_s.at[5], q_r.at[5], partner)
    ds_copy.start()

    def backward(i, total_score):
        at = pl.ds(pl.multiple_of(i * 256, 256), 256)
        at_up = pl.ds(pl.multiple_of(i * 256 + FF, 256), 256)
        h = mm(rg[...].reshape(256, D), wd[at, :], NT)
        a = (h * dsl[:, at]).astype(BF16)
        b = (h * act[:, at]).astype(BF16)
        gg[:, at] = a
        ug[:, at] = b
        pair[:, at] = (gate * a.astype(F32)).astype(BF16)
        pair[:, at_up] = (gate * b.astype(F32)).astype(BF16)
        return total_score + jnp.sum(h * hid[:, at], axis=1, keepdims=True)

    score = lax.fori_loop(0, 3, backward, jnp.zeros((256, 1), F32))
    pair_copy = remote(pair, ppair, q_s.at[6], q_r.at[6], partner)
    pair_copy.start()
    stile[...] = jnp.broadcast_to(score.astype(BF16).astype(F32), (256, 128)).reshape(NE, 8, 128)
    pltpu.make_async_copy(stile.at[where_from(0)[0]], sbuf.at[me_e], sc_r).start()

    def send_score(k):
        n, to = where_from(k)
        remote(stile.at[n], sbuf.at[me_e], sc_s, sc_r, (me_d, to)).start()

    others(NE, send_score)

    ht_copy.wait_recv()
    ds_copy.wait_recv()

    def my_rows(ref, j):
        o = lax.rem(x + j, NX)
        return ref[pl.ds(pl.multiple_of(192 * o + 96 * core, 32), 96), :]

    def down_part(i, carry):
        at = pl.ds(pl.multiple_of(i * 512, 512), 512)
        mine = jnp.concatenate([my_rows(ht, j) for j in range(4)], axis=0)
        theirs = jnp.concatenate([my_rows(pht, j) for j in range(4)], axis=0)
        out = mm(mine, ds[:, at]) + mm(theirs, pds[:, at])
        for j in range(4):
            g2[j, :, at] = out[96 * j : 96 * j + 96].astype(BF16)
        return carry

    lax.fori_loop(0, 4, down_part, 0)
    half = [
        remote(g2.at[2, pl.ds(0, 48)], ra2, h_s.at[0], h_r.at[0], right),
        remote(g2.at[2, pl.ds(48, 48)], rb2, h_s.at[1], h_r.at[1], left),
        remote(g1.at[2, pl.ds(0, 128)], ra1, h_s.at[2], h_r.at[2], right),
        remote(g1.at[2, pl.ds(128, 128)], rb1, h_s.at[3], h_r.at[3], left),
    ]
    half[0].start()
    half[1].start()
    for c in cuts:
        c.wait_recv()
    pair_copy.wait_recv()

    def pair_part(j):
        o = lax.rem(x + j, NX)
        col = pl.ds(pl.multiple_of(512 * o + 256 * core, 256), 256)

        def one(i, carry):
            at = pl.ds(pl.multiple_of(i * 512, 512), 512)
            out = mm(rt[:, :, :, col].reshape(256, 256), pair[:, at], TN)
            out = out + mm(pt[o].reshape(256, 256), ppair[:, at], TN)
            g1[j, :, at] = out.astype(BF16)
            return carry

        lax.fori_loop(0, 3, one, 0)

    pair_part(2)
    half[2].start()
    half[3].start()
    pair_part(1)
    pair_part(3)
    pair_part(0)

    drain(sbuf, sc_r)
    scores = jnp.zeros((8, 128), F32)
    for e in range(NE):
        scores = scores + jnp.where(lane8 == e, sbuf[e], 0.0)
    grad3 = jnp.zeros((TOK, 128), F32)
    for slot in range(CAP):
        grad3 = grad3 + jnp.where(
            rank == slot, jnp.broadcast_to(scores[slot : slot + 1, :], (TOK, 128)), 0.0
        )
    g = NE * grad3 * dens[3]
    h3 = g - dens[3] * jnp.sum(g, axis=1, keepdims=True)
    atile[...] = jnp.broadcast_to(jnp.sum(h3, axis=0, keepdims=True), (8, 128))
    plane(lambda e: atile, abuf.at[me_e], a_s, a_r)

    for b in range(4):
        at = slice(512 * b, 512 * b + 512)
        out = mm(gg[...], wg[at, :], NT) + mm(ug[...], wu[at, :], NT)
        rows = 8 * (b // 2)
        cut = slice(512 * (b % 2), 512 * (b % 2) + 512)
        bsend[:, rows : rows + 8, cut] = out.reshape(NE, 8, 512).astype(BF16)

    def send_back(k):
        n, to = where_from(k)
        remote(bsend.at[n], ret.at[me_e], ret_s, ret_r, (me_d, to)).start()

    pltpu.make_async_copy(bsend.at[where_from(0)[0]], ret.at[me_e], ret_r).start()
    lax.fori_loop(1, 16, lambda k, c: (send_back(k), c)[1], 0)

    gates_hi = gates.astype(BF16).astype(F32)
    ex_i, ex_j = iota((128, 512), 0), iota((128, 512), 1)
    spread = ((ex_i < NE) & (ex_j // 16 == ex_i)).astype(BF16)
    wide = mm(
        jnp.concatenate([rank, gates_hi, gates - gates_hi], axis=0).astype(BF16), spread
    )
    k16 = lax.rem(iota((TOK, 512), 1), 16)
    rank_w = wide[0:TOK].astype(jnp.int32)
    parts = []
    for m in (rank_w == k16, rank_w == k16 - 8):
        parts += [jnp.where(m, wide[TOK : 2 * TOK], 0.0), jnp.where(m, wide[2 * TOK :], 0.0)]
    weights = jnp.concatenate(parts, axis=0).astype(BF16)

    drain(abuf, a_r)
    btile[...] = jnp.sum(abuf[...], axis=0)
    pltpu.make_async_copy(btile, bbuf.at[me_d], b_r).start()
    others(
        ND,
        lambda k: remote(
            btile, bbuf.at[me_d], b_s, b_r, (lax.rem(me_d + k, ND), me_e)
        ).start(),
    )
    early = [
        remote(g2.at[1, pl.ds(48, 48)], rc2.at[pl.ds(48, 48)], n_s.at[0], n_r.at[0], right),
        remote(g2.at[3, pl.ds(0, 48)], rd2.at[pl.ds(0, 48)], n_s.at[1], n_r.at[1], left),
        remote(g1.at[1, pl.ds(128, 128)], rc1.at[pl.ds(128, 128)], n_s.at[2], n_r.at[2], right),
        remote(g1.at[3, pl.ds(0, 128)], rd1.at[pl.ds(0, 128)], n_s.at[3], n_r.at[3], left),
    ]
    for c in early:
        c.start()

    drain(bbuf, b_r)
    v = jnp.sum(bbuf[...], axis=0)
    first32 = lane8 < NE
    u = mm(jnp.where(first32, v / cols[16:24, :], 0.0), gram[1], exact=True)
    s = mm(jnp.where(first32, u / cols[8:16, :], 0.0), gram[0], exact=True)
    qv = quot[2] * v[0:1, :]
    h2 = h3 - qv + dens[2] * jnp.sum(qv, axis=1, keepdims=True)
    qu = quot[1] * u[0:1, :]
    h1 = h2 - qu + dens[1] * jnp.sum(qu, axis=1, keepdims=True)
    lgrad = (h1 - quot[0] * s[0:1, :]).astype(BF16)[:, :NE]
    router_t = mm(lgrad, tokens[...], TN)
    for p in range(NE):
        h, b = p % 2, p // 2
        rsend[p] = router_t[16 * h : 16 * h + 16, 128 * b : 128 * b + 128]
    plane(lambda e: rsend.at[e], rrecv.at[me_e], rs_s, rs_r)
    lax.fori_loop(16, NE, lambda k, c: (send_back(k), c)[1], 0)
    router_in = mm(lgrad, rw[...], NT)

    def add_rows(n, rows, terms, out):
        def one(i, c):
            at = pl.ds(pl.multiple_of(i * rows, rows), rows)
            out(at, functools.reduce(lambda a, b: a + b, [t(at).astype(F32) for t in terms]))
            return c

        lax.fori_loop(0, n // rows, one, 0)

    def put(ref, j, base):
        def f(at, value):
            ref[j, pl.ds(pl.multiple_of(at.start + base, 16), at.size), :] = value.astype(BF16)
        return f

    def take(ref, j, base):
        return lambda at: ref[j, pl.ds(pl.multiple_of(at.start + base, 16), at.size), :]

    for c in half:
        c.wait_recv()
    add_rows(48, 48, [take(g2, 1, 0), lambda at: ra2[at, :]], put(g2, 1, 0))
    add_rows(48, 48, [take(g2, 3, 48), lambda at: rb2[at, :]], put(g2, 3, 48))
    add_rows(128, 32, [take(g1, 1, 0), lambda at: ra1[at, :]], put(g1, 1, 0))
    add_rows(128, 32, [take(g1, 3, 128), lambda at: rb1[at, :]], put(g1, 3, 128))
    late = [
        remote(g2.at[1, pl.ds(0, 48)], rc2.at[pl.ds(0, 48)], m_s.at[0], m_r.at[0], right),
        remote(g2.at[3, pl.ds(48, 48)], rd2.at[pl.ds(48, 48)], m_s.at[1], m_r.at[1], left),
        remote(g1.at[1, pl.ds(0, 128)], rc1.at[pl.ds(0, 128)], m_s.at[2], m_r.at[2], right),
        remote(g1.at[3, pl.ds(128, 128)], rd1.at[pl.ds(128, 128)], m_s.at[3], m_r.at[3], left),
    ]
    late[0].start()
    late[1].start()

    drain(rrecv, rs_r)
    dsum[...] = jnp.sum(rrecv[...], axis=0)
    pltpu.make_async_copy(dsum, drecv.at[me_d], d_r).start()
    others(
        ND,
        lambda k: remote(
            dsum, drecv.at[me_d], d_s, d_r, (lax.rem(me_d + k, ND), me_e)
        ).start(),
    )
    late[2].start()
    late[3].start()
    drain(drecv, d_r)
    fin[...] = jnp.sum(drecv[...], axis=0)
    plane(lambda e: fin, router_out.at[me_e], o_s, o_r)

    drain(ret, ret_r)
    mixed = mm(weights, ret[...].reshape(512, 1024))
    gt_out[:, 0:1024] = (mixed[0:24] + mixed[24:48] + router_in[:, 0:1024]).astype(BF16)
    gt_out[:, 1024:2048] = (mixed[48:72] + mixed[72:96] + router_in[:, 1024:2048]).astype(BF16)

    for c in early + late:
        c.wait_recv()

    def store(ref):
        def f(at, value):
            ref[at, :] = value.astype(BF16)
        return f

    add_rows(
        96, 48, [take(g2, 0, 0), lambda at: rc2[at, :], lambda at: rd2[at, :]], store(down_out)
    )
    add_rows(
        256, 32, [take(g1, 0, 0), lambda at: rc1[at, :], lambda at: rd1[at, :]], store(pair_out)
    )
    drain(router_out, o_r)

    for c in t_dn + t_up + g_dn + g_up + y_copies + cuts + half + early + late:
        c.wait_send()
    for c in (logit_pair, ht_copy, ds_copy, pair_copy):
        c.wait_send()
    drain(rkbuf.at[pl.ds(0, 7)], rk_s)
    drain(lall.at[0, 0, pl.ds(0, NE - 1)], lg_s)
    drain(lall.at[0, pl.ds(0, NX - 1)], x_s)
    drain(gbuf.at[pl.ds(0, NE - 1)], g_s)
    drain(ret.at[pl.ds(0, NE - 1)], ret_s)
    drain(sbuf.at[pl.ds(0, NE - 1)], sc_s)
    drain(abuf.at[pl.ds(0, NE - 1)], a_s)
    drain(bbuf.at[pl.ds(0, ND - 1)], b_s)
    drain(rrecv.at[pl.ds(0, NE - 1)], rs_s)
    drain(drecv.at[pl.ds(0, ND - 1)], d_s)
    drain(router_out.at[pl.ds(0, NE - 1)], o_s)


def moe(*args):
    dma = pltpu.SemaphoreType.DMA
    V = pltpu.VMEM
    hbm = pl.BlockSpec(memory_space=pl.ANY)
    return pl.pallas_call(
        moe_kernel,
        name="moe",
        out_shape=(
            jax.ShapeDtypeStruct((TOK, D), BF16),
            jax.ShapeDtypeStruct((256, 2 * FF), BF16),
            jax.ShapeDtypeStruct((96, D), BF16),
            jax.ShapeDtypeStruct((NE, 16, 128), F32),
        ),
        in_specs=[VM] * 4 + [hbm] * 3,
        out_specs=(VM,) * 4,
        scratch_shapes=[
            V((D, FF), BF16), V((D, FF), BF16), V((FF, D), BF16),
            V((8, 128), F32), V((8, 8, 128), F32), V((8, 8, 128), F32),
            V((2, NX, NE, 8, 128), F32), V((8, 256, 128), F32),
            V((24, 128), F32), V((2, 128, 128), F32), V((8, 128), F32), V((NE, 8, 128), F32),
            V((8, TOK, D), BF16), V((8, TOK, D), BF16),
            V((4, 4, 16, D), BF16), V((4, 4, 16, D), BF16),
            V((4, 4, 16, D), BF16), V((4, 4, 16, D), BF16),
            V((4, 4, 4, 16, 256), BF16),
            V((256, FF), F32), V((256, FF), F32), V((256, FF), F32),
            V((FF, 256), BF16), V((FF, 256), BF16),
            V((256, D), BF16), V((256, D), BF16),
            V((256, FF), BF16), V((256, FF), BF16),
            V((256, 2 * FF), BF16), V((256, 2 * FF), BF16),
            V((4, 256, 2 * FF), BF16), V((4, 96, D), BF16),
            V((128, 2 * FF), BF16), V((48, D), BF16),
            V((128, 2 * FF), BF16), V((48, D), BF16),
            V((256, 2 * FF), BF16), V((96, D), BF16),
            V((256, 2 * FF), BF16), V((96, D), BF16),
            V((NE, 16, 1024), BF16), V((NE, 16, 1024), BF16),
            V((NE, 8, 128), F32), V((NE, 8, 128), F32),
            V((8, 128), F32), V((NE, 8, 128), F32),
            V((8, 128), F32), V((ND, 8, 128), F32),
            V((NE, 16, 128), F32), V((NE, 16, 128), F32),
            V((16, 128), F32), V((ND, 16, 128), F32), V((16, 128), F32),
            dma((3,)),
            dma((8,)), dma((8,)), dma((8,)), dma((8,)),
            dma((4, 4)), dma((4, 4)), dma((4, 4)), dma((4, 4)),
            dma((7,)), dma((7,)),
            dma((4,)), dma((4,)), dma((4,)), dma((4,)), dma((4,)), dma((4,)),
        ]
        + [dma] * 24,
        compiler_params=pltpu.CompilerParams(
            collective_id=0, has_side_effects=True, vmem_limit_bytes=61 * 1024 * 1024
        ),
    )(*args)


def write_kernel(gt, pair, down, router, gt_o, router_o, gate_o, up_o, down_o):
    gt_o[...] = gt[...]
    gate_o[0] = pair[:, 0:FF]
    up_o[0] = pair[:, FF : 2 * FF]
    down_o[0] = down[...]
    for b in range(16):
        t = jnp.concatenate([router[2 * b], router[2 * b + 1]], axis=0)
        router_o[128 * b : 128 * b + 128, :] = t.T


def write(*args):
    return pl.pallas_call(
        write_kernel,
        name="write",
        out_shape=(
            jax.ShapeDtypeStruct((TOK, D), BF16),
            jax.ShapeDtypeStruct((D, NE), F32),
            jax.ShapeDtypeStruct((1, 256, FF), BF16),
            jax.ShapeDtypeStruct((1, 256, FF), BF16),
            jax.ShapeDtypeStruct((1, 96, D), BF16),
        ),
        in_specs=[VM] * 4,
        out_specs=(VM,) * 5,
    )(*args)


def per_device(tokens, out_grad, expert_ids, router_weight, w_gate, w_up, w_down):
    gt, pair, down, router = moe(
        tokens, out_grad, expert_ids, router_weight, w_gate, w_up, w_down
    )
    return write(gt, pair, down, router)


def solution(mesh):
    in_specs = (
        P(("dp", "expert"), None), P(("dp", "expert"), None), P(("dp", "expert"), None), P(),
        P("expert", None, None), P("expert", None, None), P("expert", None, None),
    )
    out_specs = (
        P(("dp", "expert"), None), P(),
        P("expert", "dp", None), P("expert", "dp", None), P("expert", "dp", None),
    )
    return jax.shard_map(
        per_device, mesh=mesh, in_specs=in_specs, out_specs=out_specs, check_vma=False
    )
```

time: 182 us -> 116 us (0.64)
  Pallas kernels: 148 us -> 110 us
  matrix products: 20.5 us -> 0 us
  local copies, waits for them, and re-layouts: 12.3 us -> 5.49 us
    pallas_call x2, Pallas kernels: 148 us -> 110 us  [the longest x1 107 us: moe(): pl.pallas_call(moe_kernel, name='moe', out_shape=(jax.ShapeDtypeStruct((T...]
    dot_general x10 -> x0, matrix products: 20.5 us -> none  [the longest x2 7.39 us: column_product(): lax.dot_general(a, b, (((0,), (0,)), ((), ())), preferred_element_type=F32)]
    unnamed x14 -> x2, local copies, waits for them, and re-layouts: 6.31 us -> 3.25 us
    broadcast_in_dim x2 -> x0, local copies, waits for them, and re-layouts: 2.81 us -> none  [the longest x1 2.04 us: per_device(): return (gt, grad_router, pair[None, :, :FF], pair[None, :, FF:], down[None])]
    pallas_call x0 -> x1, local copies, waits for them, and re-layouts: none -> 2.24 us  [write(): pl.pallas_call(write_kernel, name='write', out_shape=(jax.ShapeDtypeStruc...]
    pad x3 -> x0, local copies, waits for them, and re-layouts: 1.83 us -> none  [the longest x1 0.62 us: per_device(): logits_w = jnp.pad(logits, ((0, 0), (0, 96)))]
where the time goes in v2:
time: 116 us
  Pallas kernels  110 us (95%)
  local copies, waits for them, and re-layouts  5.49 us (5%)
    pallas_call x1, Pallas kernels, moe(): pl.pallas_call(moe_kernel, name='moe', out_shape=(jax.ShapeDtypeStruct((T...  107 us
    unnamed x2, local copies, waits for them, and re-layouts  3.25 us
    pallas_call x1, Pallas kernels, write(): pl.pallas_call(write_kernel, name='write', out_shape=(jax.ShapeDtypeStruc...  3 us

profile of v2, /device:TPU:1, one launch (start us, length us, event | category | flops | bytes accessed | tf_op | source)
XLA Modules:
  0.0 115.8 jit_solution(18441981094336377559)
XLA Ops:
  0.6 1.4 %copy.12.ids = s32[24,8]{1,0:T(8,128)} copy(s32[24,8]{0,1:T(8,128)} %param.9) | data formatting | bytes 1536 | tf_op args[2]
  2.0 1.9 %copy.13.rw = bf16[2048,32]{1,0:T(8,128)(2,1)} copy(bf16[2048,32]{0,1:T(8,128)(2,1)} %param.10) | data formatting | bytes 262144 | tf_op args[3]
  3.9 106.7 %moe.1 = (bf16[24,2048]{1,0:T(8,128)(2,1)}, bf16[256,1536]{1,0:T(8,128)(2,1)}, bf16[96,2048]{1,0:T(8,128)(2,1)}, f32[32,16,128]{2,1,0:T(8,128)}) custom-call(bf16[24,2048]{1,0:T(8,128)(2,1)} %tokens.1, bf16[24,2048]{1,0:T(8,128)(2,1)} %grads.1, s32[24,8]{1,0:T(8,128)} %copy.12.ids, bf16[2048,32]{1,0:T(8,128)(2,1)} %copy.13.rw, bf16[1,2048,768]{2,1,0:T(8,128)(2,1)} %wg_hbm.1, ...), custom_call_target="tpu_custom_call" | custom-call | tf_op jit(solution)/shard_map/moe/pallas_call | solution.py:598
  110.6 3.0 %write.1 = (bf16[24,2048]{1,0:T(8,128)(2,1)}, f32[2048,32]{1,0:T(8,128)}, bf16[1,256,768]{2,1,0:T(8,128)(2,1)}, bf16[1,256,768]{2,1,0:T(8,128)(2,1)}, bf16[1,96,2048]{2,1,0:T(8,128)(2,1)}) custom-call(bf16[24,2048]{1,0:T(8,128)(2,1)} %get-tuple-element.9.gt, bf16[256,1536]{1,0:T(8,128)(2,1)} %get-tuple-element.10.pair, ...), custom_call_target="tpu_custom_call" | custom-call | tf_op jit(solution)/shard_map/write/pallas_call | solution.py:658
  113.6 2.2 %copy.14 = f32[2048,32]{0,1:T(8,128)} copy(f32[2048,32]{1,0:T(8,128)} %get-tuple-element.14) | data formatting | bytes 524288 | tf_op jit(solution)/shard_map/write/pallas_call | solution.py:658

commit v3 on v2

--- a/solution.py
+++ b/solution.py
@@ -44,23 +44,6 @@
     lax.fori_loop(1, n, lambda k, c: (body(k), c)[1], 0)
 
 
-def greet(me_d, me_e):
-    barrier = pltpu.get_barrier_semaphore()
-    others(
-        NE,
-        lambda k: pl.semaphore_signal(
-            barrier, inc=1, device_id=(me_d, lax.rem(me_e + k, NE)), device_id_type=MESH
-        ),
-    )
-    others(
-        ND,
-        lambda k: pl.semaphore_signal(
-            barrier, inc=1, device_id=(lax.rem(me_d + k, ND), me_e), device_id_type=MESH
-        ),
-    )
-    pl.semaphore_wait(barrier, NE - 1 + ND - 1)
-
-
 def own_state(logits, cols):
     lane = iota((TOK, 128), 1)
     d = jnp.where(lane < NE, jnp.exp(logits), 0.0)
@@ -87,11 +70,11 @@
 def moe_kernel(
     tokens, grads, ids, rw, wg_hbm, wu_hbm, wd_hbm,
     gt_out, pair_out, down_out, router_out,
-    wg, wu, wd, packed, rk, rkbuf, lall, dd, cols, gram, gtile, gbuf,
+    wg, wu, wd, zmsg, zin, et, eg, qt, qg, lall, dd, db, cols, gram, gtile, gbuf,
     zt, zg, yt, yg, rt, rg, pt, hid, act, dsl, ht, pht, ds, pds, gg, ug, pair, ppair,
     g1, g2, ra1, ra2, rb1, rb2, rc1, rc2, rd1, rd2,
     bsend, ret, stile, sbuf, atile, abuf, btile, bbuf, rsend, rrecv, dsum, drecv, fin,
-    w_sem, zs_t, zr_t, zs_g, zr_g, ys_t, yr_t, ys_g, yr_g, q_s, q_r, h_s, h_r, n_s, n_r, m_s, m_r,
+    w_sem, zs_t, zr_t, zs_g, zr_g, ys_t, yr_t, ys_g, yr_g, es_t, er_t, es_g, er_g, q_s, q_r, h_s, h_r, n_s, n_r, m_s, m_r,
     lg_s, lg_r, rk_s, rk_r, x_s, x_r, p_s, p_r, g_s, g_r, ret_s, ret_r, sc_s, sc_r,
     a_s, a_r, b_s, b_r, rs_s, rs_r, d_s, d_r, o_s, o_r,
 ):
@@ -122,32 +105,34 @@
     z_up = (me_d, y * 8 + lax.rem(z + 1, 8))
     z_down = (me_d, y * 8 + lax.rem(z + 7, 8))
 
-    lane24 = iota((TOK, 128), 1)
     lane8, sub8 = iota((8, 128), 1), iota((8, 128), 0)
     logits = jnp.concatenate(
-        [mm(tokens[...], rw[...]), jnp.zeros((TOK, 96), F32)], axis=1
-    )
-    packed[...] = (
+        [mm(tokens[...], rw[...], NT), jnp.zeros((TOK, 96), F32)], axis=1
+    )
+    packed = (
         logits[0:8] + pltpu.roll(logits[8:16], 32, 1) + pltpu.roll(logits[16:24], 64, 1)
     )
-    picked = jnp.zeros((TOK, 128), F32)
+    picked_t = jnp.zeros((128, TOK), F32)
     for k in range(8):
-        picked = picked + (ids[:, k : k + 1] == lane24).astype(F32)
-    before = (iota((TOK, TOK), 0) > iota((TOK, TOK), 1)).astype(BF16)
-    rank = jnp.where(picked > 0, mm(before, picked.astype(BF16)), -64.0)
+        picked_t = picked_t + (ids[k : k + 1, :] == iota((128, TOK), 0)).astype(F32)
+    picked_t = picked_t.astype(BF16)
+    row_t, col_t = iota((TOK, TOK), 0), iota((TOK, TOK), 1)
+    picked = mm((row_t == col_t).astype(BF16), picked_t, NT)
+    rank = jnp.where(picked > 0, mm((row_t > col_t).astype(BF16), picked_t, NT), -64.0)
     rank_pad = jnp.concatenate([rank, jnp.full((104, 128), -64.0, F32)], axis=0).astype(BF16)
     pi, pj = iota((64, 128), 0), iota((64, 128), 1)
     place_rows = ((lax.rem(pi, 8) < 4) & (pj == lax.rem(pi, 8) * 8 + pi // 8)).astype(BF16)
-    rk[...] = mm(place_rows, rank_pad, NT).reshape(8, 8, 128)
+    zmsg[:, 0:8, :] = mm(place_rows, rank_pad, NT).reshape(8, 8, 128)
+    zmsg[:, 8:16, :] = jnp.broadcast_to(packed[None], (8, 8, 128))
 
     pl.semaphore_wait(barrier, NE - 1 + ND - 1)
 
-    def z_ring(k):
+    def z_send(k):
         to = lax.rem(z + k, 8)
-        remote(rk.at[to], rkbuf.at[z], rk_s, rk_r, (me_d, y * 8 + to)).start()
-
-    pltpu.make_async_copy(rk.at[z], rkbuf.at[z], rk_r).start()
-    others(8, z_ring)
+        remote(zmsg.at[to], zin.at[z], rk_s, rk_r, (me_d, y * 8 + to)).start()
+
+    pltpu.make_async_copy(zmsg.at[z], zin.at[z], rk_r).start()
+    others(8, z_send)
 
     def z_copy(own, buf, ss, rs, k, sign):
         at = lambda n: (8 + sign * n) % 8
@@ -163,68 +148,85 @@
     t_dn[0].start()
     t_up[0].start()
 
-    def plane(src, dst, send, recv):
-        pltpu.make_async_copy(src(me_e), dst, recv).start()
-
-        def go(k):
-            to = lax.rem(me_e + k, NE)
-            remote(src(to), dst, send, recv, (me_d, to)).start()
-
-        others(NE, go)
-
-    plane(lambda e: packed, lall.at[core, x, me_e], lg_s, lg_r)
     g_dn[0].start()
     g_up[0].start()
 
-    drain(rkbuf, rk_r)
-
-    def choose(zs, half):
+    def hot(ref, at, yy):
+        row = ref[at, yy : yy + 1, :]
+        return (jnp.broadcast_to(row, (8, 128)) == sub8.astype(F32)).astype(F32)
+
+    def choose(at, half):
+        none = jnp.zeros((8, 128), F32)
         parts = []
         for yy in range(4):
-            row = rkbuf[zs, yy : yy + 1, :]
-            hot = (jnp.broadcast_to(row, (8, 128)) == sub8.astype(F32)).astype(F32)
-            none = jnp.zeros((8, 128), F32)
-            parts += [hot, none] if half == 0 else [none, hot]
+            one = hot(zin, at, yy)
+            parts += [one, none] if half == 0 else [none, one]
         return jnp.concatenate(parts, axis=0).astype(BF16)[:, :TOK]
 
     y_copies = []
 
-    def y_phase(j, own, buf, send_buf, recv_buf, ss, rs):
-        first = own[...] if j == 0 else buf[j]
-        out = mm(choose(lax.rem(z + j, 8), 0), first)
-        out = out + mm(choose(lax.rem(z + 7 - j, 8), 1), buf[7 - j])
-        send_buf[j] = out.astype(BF16).reshape(4, 16, D)
+    def y_send(src, dst, ss, rs, j):
         for m in range(1, 4):
             to = lax.rem(y + m, 4)
-            c = remote(
-                send_buf.at[j, to], recv_buf.at[y, j], ss.at[j, m], rs.at[j, m],
-                (me_d, to * 8 + z),
-            )
+            c = remote(src(to), dst, ss.at[j, m], rs.at[j, m], (me_d, to * 8 + z))
             c.start()
             y_copies.append(c)
-        c = pltpu.make_async_copy(send_buf.at[j, y], recv_buf.at[y, j], rs.at[j, 0])
+        pltpu.make_async_copy(src(y), dst, rs.at[j, 0]).start()
+
+    def y_pair(j, buf, send_buf, recv_buf, ss, rs):
+        out = mm(choose(lax.rem(z + 8 - j, 8), 0), buf[8 - j])
+        out = out + mm(choose(lax.rem(z + j, 8), 1), buf[j])
+        send_buf[j] = out.astype(BF16).reshape(4, 16, D)
+        y_send(lambda to: send_buf.at[j, to], recv_buf.at[y, j], ss, rs, j)
+
+    def y_single(n, block, ref, at, send_buf, recv_buf, ss, rs):
+        pick = jnp.concatenate([hot(ref, at, yy) for yy in range(4)], axis=0)
+        out = mm(pick.astype(BF16)[:, :TOK], block)
+        for yy in range(4):
+            rows = out[8 * yy : 8 * yy + 8]
+            send_buf[n, yy] = jnp.concatenate([rows[:, :1024], rows[:, 1024:]], axis=0).astype(BF16)
+        y_send(lambda to: send_buf.at[n, to], recv_buf.at[y, n], ss, rs, n)
+
+    def y_wait(recv_buf, rs, one_buf, one_rs):
+        for m in range(4):
+            for j in range(1, 4):
+                drain(recv_buf.at[0, 0], rs.at[j, m])
+            for n in range(2):
+                drain(one_buf.at[0, 0], one_rs.at[n, m])
+        for yy in range(4):
+            parts = []
+            for n in range(2):
+                a = one_buf[yy, n].astype(F32)
+                parts.append(jnp.concatenate([a[0:8], a[8:16]], axis=1))
+            recv_buf[yy, 0] = jnp.concatenate(parts, axis=0).astype(BF16)
+
+    def arrive(down, up, k):
+        if k < len(down):
+            down[k].wait_recv()
+            if k + 1 < len(down):
+                down[k + 1].start()
+        if k < len(up):
+            up[k].wait_recv()
+            if k + 1 < len(up):
+                up[k + 1].start()
+
+    y_single(0, tokens[...], zmsg, z, et, qt, es_t, er_t)
+    y_single(0, grads[...], zmsg, z, eg, qg, es_g, er_g)
+
+    drain(zin, rk_r)
+    own_z = zin.at[:, pl.ds(8, 8), :]
+    own_rows = lall.at[core, x, pl.ds(pl.multiple_of(y * 8, 8), 8)]
+    pltpu.make_async_copy(own_z, own_rows, lg_r).start()
+    lg_copies = []
+    for m in range(1, 4):
+        c = remote(
+            own_z, own_rows, lg_s.at[m - 1], lg_r, (me_d, lax.rem(y + m, 4) * 8 + z)
+        )
         c.start()
-
-    def y_wait(recv_buf, rs):
-        for j in range(4):
-            for m in range(4):
-                drain(recv_buf.at[0, 0], rs.at[j, m])
-
-    t_dn[0].wait_recv()
-    t_dn[1].start()
-    t_up[0].wait_recv()
-    t_up[1].start()
-    y_phase(0, tokens, zt, yt, rt, ys_t, yr_t)
-    g_dn[0].wait_recv()
-    g_dn[1].start()
-    g_up[0].wait_recv()
-    g_up[1].start()
-    t_dn[1].wait_recv()
-    t_dn[2].start()
-    t_up[1].wait_recv()
-    t_up[2].start()
-    y_phase(1, tokens, zt, yt, rt, ys_t, yr_t)
-
+        lg_copies.append(c)
+
+    arrive(t_dn, t_up, 0)
+    y_pair(1, zt, yt, rt, ys_t, yr_t)
     drain(lall.at[core, x], lg_r)
     others(
         NX,
@@ -232,64 +234,57 @@
             lall.at[core, x], lall.at[core, x], x_s, x_r, (lax.rem(x + k, NX) * 2 + core, me_e)
         ).start(),
     )
-
-    g_dn[1].wait_recv()
-    g_dn[2].start()
-    g_up[1].wait_recv()
-    g_up[2].start()
-    t_dn[2].wait_recv()
-    t_dn[3].start()
-    t_up[2].wait_recv()
-    y_phase(2, tokens, zt, yt, rt, ys_t, yr_t)
-    y_phase(0, grads, zg, yg, rg, ys_g, yr_g)
-    g_dn[2].wait_recv()
-    g_up[2].wait_recv()
-    g_up[3].start()
-    t_dn[3].wait_recv()
-    y_phase(3, tokens, zt, yt, rt, ys_t, yr_t)
-    y_phase(1, grads, zg, yg, rg, ys_g, yr_g)
-    y_phase(2, grads, zg, yg, rg, ys_g, yr_g)
+    arrive(g_dn, g_up, 0)
+    y_pair(1, zg, yg, rg, ys_g, yr_g)
+    arrive(t_dn, t_up, 1)
+    y_pair(2, zt, yt, rt, ys_t, yr_t)
+    arrive(g_dn, g_up, 1)
+    y_pair(2, zg, yg, rg, ys_g, yr_g)
+    arrive(t_dn, t_up, 2)
+    y_pair(3, zt, yt, rt, ys_t, yr_t)
     drain(lall.at[core, pl.ds(0, NX - 1)], x_r)
     logit_pair = remote(lall.at[core], lall.at[core], p_s, p_r, partner)
     logit_pair.start()
-    g_up[3].wait_recv()
-    y_phase(3, grads, zg, yg, rg, ys_g, yr_g)
+    arrive(g_dn, g_up, 2)
+    far = lax.rem(z + 4, 8)
+    arrive(t_dn, t_up, 3)
+    y_single(1, zt[4], zin, far, et, qt, es_t, er_t)
+    y_pair(3, zg, yg, rg, ys_g, yr_g)
     drain(lall.at[1 - core], p_r)
 
-    valid = iota((256, 128), 1) < 96
+    valid = iota((1024, 128), 1) < 96
     li, lj = iota((128, 128), 0), iota((128, 128), 1)
     fold = (lax.rem(li, 32) == lax.rem(lj, 32)).astype(F32)
     block = (li // 32 == lj // 32).astype(F32)
+    block_h = block.astype(BF16)
 
     def rows_of(a):
-        return jnp.sum(a.reshape(32, 8, 128), axis=0)
-
-    def first(i, acc):
-        d0 = jnp.where(valid, jnp.exp(lall[i // NX, lax.rem(i, NX)].reshape(256, 128)), 0.0)
-        dd[i] = d0
-        return acc + rows_of(d0)
-
-    acc = lax.fori_loop(0, 8, first, jnp.zeros((8, 128), F32))
-    pad = jnp.where(valid, 0.0, 1.0)
+        return jnp.sum(jnp.sum(a.reshape(8, 16, 8, 128), axis=1), axis=0)
 
     def total(acc):
         one = jnp.broadcast_to(jnp.sum(acc, axis=0, keepdims=True), (8, 128))
         return mm(one, fold, exact=True)
 
+    acc = jnp.zeros((8, 128), F32)
+    for i in range(2):
+        d0 = jnp.where(valid, jnp.exp(lall[i].reshape(1024, 128)), 0.0)
+        dd[i] = d0
+        acc = acc + rows_of(d0)
+    pad = jnp.where(iota((1, 128), 1) < 96, 0.0, 1.0)
     c = total(acc)
     cols[0:8, :] = c
     for p in range(2):
-        def step(i, carry):
-            acc, g = carry
-            q = dd[i] / c[0:1, :]
-            d = q / (mm(q, block, exact=True) + pad)
-            dd[i] = d
-            return acc + rows_of(d), g + mm(d, d, TN, exact=True)
-
-        acc, g = lax.fori_loop(
-            0, 8, step, (jnp.zeros((8, 128), F32), jnp.zeros((128, 128), F32))
-        )
-        gram[p] = mm(mm(fold, g * block, exact=True), fold, exact=True)
+        acc = jnp.zeros((8, 128), F32)
+        inverse = 1.0 / c[0:1, :]
+        for i in range(2):
+            q = dd[i] * inverse
+            q_hi = q.astype(BF16)
+            q_lo = (q - q_hi.astype(F32)).astype(BF16)
+            d = q / (mm(q_hi, block_h) + mm(q_lo, block_h) + pad)
+            if p == 0:
+                dd[i] = d
+            db[p, i] = d.astype(BF16)
+            acc = acc + rows_of(d)
         c = total(acc)
         cols[8 * p + 8 : 8 * p + 16, :] = c
 
@@ -300,12 +295,24 @@
     for slot in range(CAP):
         one = jnp.sum(jnp.where(rank == slot, gates, 0.0), axis=0, keepdims=True)
         tile = tile + jnp.where(sub8 == slot, jnp.broadcast_to(one, (8, 128)), 0.0)
-    gtile[...] = tile
-    plane(lambda e: gtile, gbuf.at[me_e], g_s, g_r)
+    eye8 = (iota((8, 128), 0) == lane8).astype(BF16)
+    gtile[...] = mm(tile.astype(BF16), eye8, TN)[0:NE].reshape(NE, 1, 128)
+    def plane(src, dst, send, recv):
+        pltpu.make_async_copy(src(me_e), dst, recv).start()
+
+        def go(k):
+            to = lax.rem(me_e + k, NE)
+            remote(src(to), dst, send, recv, (me_d, to)).start()
+
+        others(NE, go)
+
+    plane(lambda e: gtile.at[e], gbuf.at[me_e], g_s, g_r)
+    arrive(g_dn, g_up, 3)
+    y_single(1, zg[4], zin, far, eg, qg, es_g, er_g)
 
     for c in loads:
         c.wait()
-    y_wait(rt, yr_t)
+    y_wait(rt, yr_t, qt, er_t)
     cuts = []
     for o in range(4):
         at = pl.ds(pl.multiple_of(512 * o + 256 * (1 - core), 256), 256)
@@ -336,21 +343,18 @@
         o = lax.rem(k, 8)
         j, h = o // 2, lax.rem(o, 2)
         yy = lax.rem(y + k // 8, 4)
-        zz = lax.rem(z + j - h * (2 * j + 1) + 16, 8)
+        zz = lax.rem(z + h * (j + 4 * ((4 - j) // 4)) + (1 - h) * (8 - j), 8)
         return yy * 8 + o, yy * 8 + zz
 
     drain(gbuf, g_r)
     tiles = []
     for yy in range(4):
-        for o in range(8):
-            j, h = o // 2, o % 2
-            tiles.append(gbuf[yy * 8 + lax.rem(z + (j if h == 0 else 7 - j), 8)])
-    gate = jnp.sum(
-        jnp.where(iota((256, 128), 1) == me_e, jnp.concatenate(tiles, axis=0), 0.0),
-        axis=1, keepdims=True,
-    ).astype(BF16).astype(F32)
-
-    y_wait(rg, yr_g)
+        for off in (0, 4, 7, 1, 6, 2, 5, 3):
+            one = gbuf[yy * 8 + lax.rem(z + off, 8)]
+            tiles.append(jnp.where(lane8 == sub8, jnp.broadcast_to(one, (8, 128)), 0.0))
+    gate = jnp.sum(jnp.concatenate(tiles, axis=0), axis=1, keepdims=True)
+
+    y_wait(rg, yr_g, qg, er_g)
     for b in range(4):
         at = slice(512 * b, 512 * b + 512)
         ds[:, at] = (gate * rg[:, :, :, at].reshape(256, 512).astype(F32)).astype(BF16)
@@ -372,7 +376,9 @@
     score = lax.fori_loop(0, 3, backward, jnp.zeros((256, 1), F32))
     pair_copy = remote(pair, ppair, q_s.at[6], q_r.at[6], partner)
     pair_copy.start()
-    stile[...] = jnp.broadcast_to(score.astype(BF16).astype(F32), (256, 128)).reshape(NE, 8, 128)
+    spread8 = jnp.broadcast_to(score.astype(BF16).astype(F32), (256, 128)).reshape(NE, 8, 128)
+    diag = iota((NE, 8, 128), 1) == iota((NE, 8, 128), 2)
+    stile[...] = jnp.sum(jnp.where(diag, spread8, 0.0), axis=1).reshape(NE, 1, 128)
     pltpu.make_async_copy(stile.at[where_from(0)[0]], sbuf.at[me_e], sc_r).start()
 
     def send_score(k):
@@ -401,9 +407,16 @@
     half = [
         remote(g2.at[2, pl.ds(0, 48)], ra2, h_s.at[0], h_r.at[0], right),
         remote(g2.at[2, pl.ds(48, 48)], rb2, h_s.at[1], h_r.at[1], left),
-        remote(g1.at[2, pl.ds(0, 128)], ra1, h_s.at[2], h_r.at[2], right),
-        remote(g1.at[2, pl.ds(128, 128)], rb1, h_s.at[3], h_r.at[3], left),
     ]
+    for n in range(2):
+        at = pl.ds(64 * n, 64)
+        half += [
+            remote(g1.at[2, at], ra1.at[at], h_s.at[2 * n + 2], h_r.at[2 * n + 2], right),
+            remote(
+                g1.at[2, pl.ds(128 + 64 * n, 64)], rb1.at[at],
+                h_s.at[2 * n + 3], h_r.at[2 * n + 3], left,
+            ),
+        ]
     half[0].start()
     half[1].start()
     for c in cuts:
@@ -426,14 +439,26 @@
     pair_part(2)
     half[2].start()
     half[3].start()
+    for b in range(4):
+        at = slice(512 * b, 512 * b + 512)
+        out = mm(gg[...], wg[at, :], NT) + mm(ug[...], wu[at, :], NT)
+        rows = 8 * (b // 2)
+        cut = slice(512 * (b % 2), 512 * (b % 2) + 512)
+        bsend[:, rows : rows + 8, cut] = out.reshape(NE, 8, 512).astype(BF16)
+
+    def send_back(k):
+        n, to = where_from(k)
+        remote(bsend.at[n], ret.at[me_e], ret_s, ret_r, (me_d, to)).start()
+
+    pltpu.make_async_copy(bsend.at[where_from(0)[0]], ret.at[me_e], ret_r).start()
+    lax.fori_loop(1, 5, lambda k, c: (send_back(k), c)[1], 0)
     pair_part(1)
     pair_part(3)
     pair_part(0)
 
     drain(sbuf, sc_r)
-    scores = jnp.zeros((8, 128), F32)
-    for e in range(NE):
-        scores = scores + jnp.where(lane8 == e, sbuf[e], 0.0)
+    eye32 = (iota((NE, 128), 0) == iota((NE, 128), 1)).astype(BF16)
+    scores = mm(sbuf[...].reshape(NE, 128).astype(BF16), eye32, TN)
     grad3 = jnp.zeros((TOK, 128), F32)
     for slot in range(CAP):
         grad3 = grad3 + jnp.where(
@@ -441,22 +466,9 @@
         )
     g = NE * grad3 * dens[3]
     h3 = g - dens[3] * jnp.sum(g, axis=1, keepdims=True)
-    atile[...] = jnp.broadcast_to(jnp.sum(h3, axis=0, keepdims=True), (8, 128))
+    atile[...] = jnp.sum(h3, axis=0, keepdims=True)
     plane(lambda e: atile, abuf.at[me_e], a_s, a_r)
-
-    for b in range(4):
-        at = slice(512 * b, 512 * b + 512)
-        out = mm(gg[...], wg[at, :], NT) + mm(ug[...], wu[at, :], NT)
-        rows = 8 * (b // 2)
-        cut = slice(512 * (b % 2), 512 * (b % 2) + 512)
-        bsend[:, rows : rows + 8, cut] = out.reshape(NE, 8, 512).astype(BF16)
-
-    def send_back(k):
-        n, to = where_from(k)
-        remote(bsend.at[n], ret.at[me_e], ret_s, ret_r, (me_d, to)).start()
-
-    pltpu.make_async_copy(bsend.at[where_from(0)[0]], ret.at[me_e], ret_r).start()
-    lax.fori_loop(1, 16, lambda k, c: (send_back(k), c)[1], 0)
+    lax.fori_loop(5, 16, lambda k, c: (send_back(k), c)[1], 0)
 
     gates_hi = gates.astype(BF16).astype(F32)
     ex_i, ex_j = iota((128, 512), 0), iota((128, 512), 1)
@@ -470,6 +482,11 @@
     for m in (rank_w == k16, rank_w == k16 - 8):
         parts += [jnp.where(m, wide[TOK : 2 * TOK], 0.0), jnp.where(m, wide[2 * TOK :], 0.0)]
     weights = jnp.concatenate(parts, axis=0).astype(BF16)
+
+    for p in range(2):
+        dens_h = db[p].reshape(2048, 128)
+        g = mm(dens_h, dens_h, TN)
+        gram[p] = mm(mm(fold, g * block, exact=True), fold, exact=True)
 
     drain(abuf, a_r)
     btile[...] = jnp.sum(abuf[...], axis=0)
@@ -480,17 +497,23 @@
             btile, bbuf.at[me_d], b_s, b_r, (lax.rem(me_d + k, ND), me_e)
         ).start(),
     )
+    half[4].start()
+    half[5].start()
     early = [
         remote(g2.at[1, pl.ds(48, 48)], rc2.at[pl.ds(48, 48)], n_s.at[0], n_r.at[0], right),
         remote(g2.at[3, pl.ds(0, 48)], rd2.at[pl.ds(0, 48)], n_s.at[1], n_r.at[1], left),
-        remote(g1.at[1, pl.ds(128, 128)], rc1.at[pl.ds(128, 128)], n_s.at[2], n_r.at[2], right),
-        remote(g1.at[3, pl.ds(0, 128)], rd1.at[pl.ds(0, 128)], n_s.at[3], n_r.at[3], left),
     ]
-    for c in early:
+    for n in range(2):
+        up, down = pl.ds(128 + 64 * n, 64), pl.ds(64 * n, 64)
+        early += [
+            remote(g1.at[1, up], rc1.at[up], n_s.at[2 * n + 2], n_r.at[2 * n + 2], right),
+            remote(g1.at[3, down], rd1.at[down], n_s.at[2 * n + 3], n_r.at[2 * n + 3], left),
+        ]
+    for c in early[0:4]:
         c.start()
 
     drain(bbuf, b_r)
-    v = jnp.sum(bbuf[...], axis=0)
+    v = jnp.broadcast_to(jnp.sum(bbuf[...], axis=0), (8, 128))
     first32 = lane8 < NE
     u = mm(jnp.where(first32, v / cols[16:24, :], 0.0), gram[1], exact=True)
     s = mm(jnp.where(first32, u / cols[8:16, :], 0.0), gram[0], exact=True)
@@ -502,10 +525,10 @@
     router_t = mm(lgrad, tokens[...], TN)
     for p in range(NE):
         h, b = p % 2, p // 2
-        rsend[p] = router_t[16 * h : 16 * h + 16, 128 * b : 128 * b + 128]
+        rsend[p] = router_t[16 * h : 16 * h + 16, 128 * b : 128 * b + 128].astype(BF16)
     plane(lambda e: rsend.at[e], rrecv.at[me_e], rs_s, rs_r)
     lax.fori_loop(16, NE, lambda k, c: (send_back(k), c)[1], 0)
-    router_in = mm(lgrad, rw[...], NT)
+    router_in = mm(lgrad, rw[...])
 
     def add_rows(n, rows, terms, out):
         def one(i, c):
@@ -535,11 +558,8 @@
         remote(g1.at[1, pl.ds(0, 128)], rc1.at[pl.ds(0, 128)], m_s.at[2], m_r.at[2], right),
         remote(g1.at[3, pl.ds(128, 128)], rd1.at[pl.ds(128, 128)], m_s.at[3], m_r.at[3], left),
     ]
-    late[0].start()
-    late[1].start()
-
     drain(rrecv, rs_r)
-    dsum[...] = jnp.sum(rrecv[...], axis=0)
+    dsum[...] = jnp.sum(rrecv[...].astype(F32), axis=0).astype(BF16)
     pltpu.make_async_copy(dsum, drecv.at[me_d], d_r).start()
     others(
         ND,
@@ -547,10 +567,12 @@
             dsum, drecv.at[me_d], d_s, d_r, (lax.rem(me_d + k, ND), me_e)
         ).start(),
     )
-    late[2].start()
-    late[3].start()
+    early[4].start()
+    early[5].start()
+    for c in late:
+        c.start()
     drain(drecv, d_r)
-    fin[...] = jnp.sum(drecv[...], axis=0)
+    fin[...] = jnp.sum(drecv[...].astype(F32), axis=0).astype(BF16)
     plane(lambda e: fin, router_out.at[me_e], o_s, o_r)
 
     drain(ret, ret_r)
@@ -574,12 +596,11 @@
     )
     drain(router_out, o_r)
 
-    for c in t_dn + t_up + g_dn + g_up + y_copies + cuts + half + early + late:
+    for c in t_dn + t_up + g_dn + g_up + y_copies + lg_copies + cuts + half + early + late:
         c.wait_send()
     for c in (logit_pair, ht_copy, ds_copy, pair_copy):
         c.wait_send()
-    drain(rkbuf.at[pl.ds(0, 7)], rk_s)
-    drain(lall.at[0, 0, pl.ds(0, NE - 1)], lg_s)
+    drain(zin.at[pl.ds(0, 7)], rk_s)
     drain(lall.at[0, pl.ds(0, NX - 1)], x_s)
     drain(gbuf.at[pl.ds(0, NE - 1)], g_s)
     drain(ret.at[pl.ds(0, NE - 1)], ret_s)
@@ -594,7 +615,7 @@
 def moe(*args):
     dma = pltpu.SemaphoreType.DMA
     V = pltpu.VMEM
-    hbm = pl.BlockSpec(memory_space=pl.ANY)
+    hbm = pl.BlockSpec(memory_space=pltpu.HBM)
     return pl.pallas_call(
         moe_kernel,
         name="moe",
@@ -602,15 +623,17 @@
             jax.ShapeDtypeStruct((TOK, D), BF16),
             jax.ShapeDtypeStruct((256, 2 * FF), BF16),
             jax.ShapeDtypeStruct((96, D), BF16),
-            jax.ShapeDtypeStruct((NE, 16, 128), F32),
+            jax.ShapeDtypeStruct((NE, 16, 128), BF16),
         ),
         in_specs=[VM] * 4 + [hbm] * 3,
         out_specs=(VM,) * 4,
         scratch_shapes=[
             V((D, FF), BF16), V((D, FF), BF16), V((FF, D), BF16),
-            V((8, 128), F32), V((8, 8, 128), F32), V((8, 8, 128), F32),
-            V((2, NX, NE, 8, 128), F32), V((8, 256, 128), F32),
-            V((24, 128), F32), V((2, 128, 128), F32), V((8, 128), F32), V((NE, 8, 128), F32),
+            V((8, 16, 128), F32), V((8, 16, 128), F32),
+            V((2, 4, 16, 1024), BF16), V((2, 4, 16, 1024), BF16),
+            V((4, 2, 16, 1024), BF16), V((4, 2, 16, 1024), BF16),
+            V((2, NX, NE, 8, 128), F32), V((2, 1024, 128), F32), V((2, 2, 1024, 128), BF16),
+            V((24, 128), F32), V((2, 128, 128), F32), V((NE, 1, 128), F32), V((NE, 1, 128), F32),
             V((8, TOK, D), BF16), V((8, TOK, D), BF16),
             V((4, 4, 16, D), BF16), V((4, 4, 16, D), BF16),
             V((4, 4, 16, D), BF16), V((4, 4, 16, D), BF16),
@@ -626,20 +649,21 @@
             V((256, 2 * FF), BF16), V((96, D), BF16),
             V((256, 2 * FF), BF16), V((96, D), BF16),
             V((NE, 16, 1024), BF16), V((NE, 16, 1024), BF16),
-            V((NE, 8, 128), F32), V((NE, 8, 128), F32),
-            V((8, 128), F32), V((NE, 8, 128), F32),
-            V((8, 128), F32), V((ND, 8, 128), F32),
-            V((NE, 16, 128), F32), V((NE, 16, 128), F32),
-            V((16, 128), F32), V((ND, 16, 128), F32), V((16, 128), F32),
+            V((NE, 1, 128), F32), V((NE, 1, 128), F32),
+            V((1, 128), F32), V((NE, 1, 128), F32),
+            V((1, 128), F32), V((ND, 1, 128), F32),
+            V((NE, 16, 128), BF16), V((NE, 16, 128), BF16),
+            V((16, 128), BF16), V((ND, 16, 128), BF16), V((16, 128), BF16),
             dma((3,)),
             dma((8,)), dma((8,)), dma((8,)), dma((8,)),
             dma((4, 4)), dma((4, 4)), dma((4, 4)), dma((4, 4)),
+            dma((2, 4)), dma((2, 4)), dma((2, 4)), dma((2, 4)),
             dma((7,)), dma((7,)),
-            dma((4,)), dma((4,)), dma((4,)), dma((4,)), dma((4,)), dma((4,)),
+            dma((6,)), dma((6,)), dma((6,)), dma((6,)), dma((4,)), dma((4,)), dma((3,)),
         ]
-        + [dma] * 24,
+        + [dma] * 23,
         compiler_params=pltpu.CompilerParams(
-            collective_id=0, has_side_effects=True, vmem_limit_bytes=61 * 1024 * 1024
+            collective_id=0, has_side_effects=True, vmem_limit_bytes=52 * 1024 * 1024
         ),
     )(*args)
 
@@ -649,9 +673,9 @@
     gate_o[0] = pair[:, 0:FF]
     up_o[0] = pair[:, FF : 2 * FF]
     down_o[0] = down[...]
-    for b in range(16):
-        t = jnp.concatenate([router[2 * b], router[2 * b + 1]], axis=0)
-        router_o[128 * b : 128 * b + 128, :] = t.T
+    for p in range(NE):
+        h, b = p % 2, p // 2
+        router_o[16 * h : 16 * h + 16, 128 * b : 128 * b + 128] = router[p].astype(F32)
 
 
 def write(*args):
@@ -660,21 +684,23 @@
         name="write",
         out_shape=(
             jax.ShapeDtypeStruct((TOK, D), BF16),
-            jax.ShapeDtypeStruct((D, NE), F32),
+            jax.ShapeDtypeStruct((NE, D), F32),
             jax.ShapeDtypeStruct((1, 256, FF), BF16),
             jax.ShapeDtypeStruct((1, 256, FF), BF16),
             jax.ShapeDtypeStruct((1, 96, D), BF16),
         ),
         in_specs=[VM] * 4,
         out_specs=(VM,) * 5,
+        compiler_params=pltpu.CompilerParams(vmem_limit_bytes=16 * 1024 * 1024),
     )(*args)
 
 
 def per_device(tokens, out_grad, expert_ids, router_weight, w_gate, w_up, w_down):
     gt, pair, down, router = moe(
-        tokens, out_grad, expert_ids, router_weight, w_gate, w_up, w_down
-    )
-    return write(gt, pair, down, router)
+        tokens, out_grad, expert_ids.T, router_weight.T, w_gate, w_up, w_down
+    )
+    gt, router, gate, up, down = write(gt, pair, down, router)
+    return gt, router.T, gate, up, down
 
 
 def solution(mesh):

time: 116 us -> 95.5 us (0.82)
  Pallas kernels: 110 us -> 91.3 us
  local copies, waits for them, and re-layouts: 5.49 us -> 3.37 us
    pallas_call x1, Pallas kernels: 107 us -> 90 us  [moe(): pl.pallas_call(moe_kernel, name='moe', out_shape=(jax.ShapeDtypeStruct((T...]
    pallas_call x1 -> x0, local copies, waits for them, and re-layouts: 2.24 us -> none  [write(): pl.pallas_call(write_kernel, name='write', out_shape=(jax.ShapeDtypeStruc...]
    pallas_call x1, Pallas kernels: 3 us -> 1.23 us  [write(): pl.pallas_call(write_kernel, name='write', out_shape=(jax.ShapeDtypeStruc...]
    unnamed x2 -> x8, local copies, waits for them, and re-layouts: 3.25 us -> 3.37 us
where the time goes in v3:
time: 95.5 us; the launch traced here: 95.3 us
  Pallas kernels  91.3 us (96%)
  local copies, waits for them, and re-layouts  3.37 us (4%)
    pallas_call x1, Pallas kernels, moe(): pl.pallas_call(moe_kernel, name='moe', out_shape=(jax.ShapeDtypeStruct((T...  90 us
    unnamed x8, local copies, waits for them, and re-layouts  3.37 us

profile of v3, /device:TPU:1, one launch (start us, length us, event | category | flops | bytes accessed | tf_op | source)
XLA Modules:
  0.0 95.3 jit_solution(518991657014356500)
XLA Ops:
  0.6 0.0 copy-start
  0.6 0.9 copy-done
  1.5 0.0 copy-start.1
  1.5 0.9 copy-done.1
  2.4 0.0 copy-start.2
  2.4 0.9 copy-done.2
  3.3 0.0 copy-start.3
  3.3 0.7 copy-done.3
  4.0 90.0 %moe.1 = (bf16[24,2048]{1,0:T(8,128)(2,1)S(1)}, bf16[256,1536]{1,0:T(8,128)(2,1)S(1)}, bf16[96,2048]{1,0:T(8,128)(2,1)S(1)}, bf16[32,16,128]{2,1,0:T(8,128)(2,1)S(1)}) custom-call(bf16[24,2048]{1,0:T(8,128)(2,1)S(1)} %copy-done.1, bf16[24,2048]{1,0:T(8,128)(2,1)S(1)} %copy-done.2, s32[8,24]{1,0:T(8,128)S(1)} %bitcast.4, bf16[32,2048]{1,0:T(8,128)(2,1)S(1)} %bitcast.3, ...), custom_call_target="tpu_custom_call" | custom-call | tf_op jit(solution)/shard_map/moe/pallas_call | solution.py:619
  94.0 1.2 %write.1 = (bf16[24,2048]{1,0:T(8,128)(2,1)}, f32[32,2048]{1,0:T(8,128)}, bf16[1,256,768]{2,1,0:T(8,128)(2,1)}, bf16[1,256,768]{2,1,0:T(8,128)(2,1)}, bf16[1,96,2048]{2,1,0:T(8,128)(2,1)}) custom-call(bf16[24,2048]{1,0:T(8,128)(2,1)S(1)} %get-tuple-element.14.gt, bf16[256,1536]{1,0:T(8,128)(2,1)S(1)} %get-tuple-element.15.pair, ...), custom_call_target="tpu_custom_call" | custom-call | tf_op jit(solution)/shard_map/write/pallas_call | solution.py:682
Async XLA Ops:
  0.6 0.9 copy-start
  1.5 0.9 copy-start.1
  2.4 0.9 copy-start.2
  3.3 0.7 copy-start.3

commit v4 on v3

--- a/solution.py
+++ b/solution.py
@@ -70,12 +70,13 @@
 def moe_kernel(
     tokens, grads, ids, rw, wg_hbm, wu_hbm, wd_hbm,
     gt_out, pair_out, down_out, router_out,
-    wg, wu, wd, zmsg, zin, et, eg, qt, qg, lall, dd, db, cols, gram, gtile, gbuf,
+    wg, wu, wd, rk_out, rk_in, rk_col, pk_out, pk_in, et, eg, qt, qg,
+    lall, dd, db, cols, gram, gcol,
     zt, zg, yt, yg, rt, rg, pt, hid, act, dsl, ht, pht, ds, pds, gg, ug, pair, ppair,
     g1, g2, ra1, ra2, rb1, rb2, rc1, rc2, rd1, rd2,
     bsend, ret, stile, sbuf, atile, abuf, btile, bbuf, rsend, rrecv, dsum, drecv, fin,
     w_sem, zs_t, zr_t, zs_g, zr_g, ys_t, yr_t, ys_g, yr_g, es_t, er_t, es_g, er_g, q_s, q_r, h_s, h_r, n_s, n_r, m_s, m_r,
-    lg_s, lg_r, rk_s, rk_r, x_s, x_r, p_s, p_r, g_s, g_r, ret_s, ret_r, sc_s, sc_r,
+    lg_s, lg_r, rc_s, rc_r, rk_s, rk_r, pk_s, pk_r, x_s, x_r, p_s, p_r, ret_s, ret_r, sc_s, sc_r,
     a_s, a_r, b_s, b_r, rs_s, rs_r, d_s, d_r, o_s, o_r,
 ):
     me_d, me_e, x, core = place()
@@ -120,18 +121,21 @@
     picked = mm((row_t == col_t).astype(BF16), picked_t, NT)
     rank = jnp.where(picked > 0, mm((row_t > col_t).astype(BF16), picked_t, NT), -64.0)
     rank_pad = jnp.concatenate([rank, jnp.full((104, 128), -64.0, F32)], axis=0).astype(BF16)
-    pi, pj = iota((64, 128), 0), iota((64, 128), 1)
-    place_rows = ((lax.rem(pi, 8) < 4) & (pj == lax.rem(pi, 8) * 8 + pi // 8)).astype(BF16)
-    zmsg[:, 0:8, :] = mm(place_rows, rank_pad, NT).reshape(8, 8, 128)
-    zmsg[:, 8:16, :] = jnp.broadcast_to(packed[None], (8, 8, 128))
+    pi, pj = iota((32, 128), 0), iota((32, 128), 1)
+    place_rows = (pj == lax.rem(pi, 4) * 8 + pi // 4).astype(BF16)
+    rk_out[...] = mm(place_rows, rank_pad, NT).reshape(8, 4, 1, 128)
+    pk_out[...] = packed
 
     pl.semaphore_wait(barrier, NE - 1 + ND - 1)
 
     def z_send(k):
         to = lax.rem(z + k, 8)
-        remote(zmsg.at[to], zin.at[z], rk_s, rk_r, (me_d, y * 8 + to)).start()
-
-    pltpu.make_async_copy(zmsg.at[z], zin.at[z], rk_r).start()
+        dev = (me_d, y * 8 + to)
+        remote(rk_out.at[to], rk_in.at[z], rk_s, rk_r, dev).start()
+        remote(pk_out, pk_in.at[z], pk_s, pk_r, dev).start()
+
+    pltpu.make_async_copy(rk_out.at[z], rk_in.at[z], rk_r).start()
+    pltpu.make_async_copy(pk_out, pk_in.at[z], pk_r).start()
     others(8, z_send)
 
     def z_copy(own, buf, ss, rs, k, sign):
@@ -143,23 +147,27 @@
 
     t_dn = [z_copy(tokens, zt, zs_t, zr_t, k, -1) for k in (1, 2, 3, 4)]
     t_up = [z_copy(tokens, zt, zs_t, zr_t, k, 1) for k in (1, 2, 3)]
-    g_dn = [z_copy(grads, zg, zs_g, zr_g, k, -1) for k in (1, 2, 3)]
-    g_up = [z_copy(grads, zg, zs_g, zr_g, k, 1) for k in (1, 2, 3, 4)]
-    t_dn[0].start()
-    t_up[0].start()
-
-    g_dn[0].start()
-    g_up[0].start()
+    g_dn, g_up = [], []
+    for h in range(2):
+        own = grads.at[:, pl.ds(1024 * h, 1024)]
+        g_dn.append(
+            [z_copy(own, zg.at[h], zs_g.at[h], zr_g.at[h], k, -1) for k in (1, 2, 3)]
+        )
+        g_up.append(
+            [z_copy(own, zg.at[h], zs_g.at[h], zr_g.at[h], k, 1) for k in (1, 2, 3, 4)]
+        )
+    for pipe in (t_dn, t_up, g_dn[0], g_up[0], g_dn[1], g_up[1]):
+        pipe[0].start()
 
     def hot(ref, at, yy):
-        row = ref[at, yy : yy + 1, :]
+        row = ref[at, yy]
         return (jnp.broadcast_to(row, (8, 128)) == sub8.astype(F32)).astype(F32)
 
     def choose(at, half):
         none = jnp.zeros((8, 128), F32)
         parts = []
         for yy in range(4):
-            one = hot(zin, at, yy)
+            one = hot(rk_in, at, yy)
             parts += [one, none] if half == 0 else [none, one]
         return jnp.concatenate(parts, axis=0).astype(BF16)[:, :TOK]
 
@@ -173,24 +181,25 @@
             y_copies.append(c)
         pltpu.make_async_copy(src(y), dst, rs.at[j, 0]).start()
 
-    def y_pair(j, buf, send_buf, recv_buf, ss, rs):
+    def y_pair(j, buf, send_buf, dst, ss, rs):
         out = mm(choose(lax.rem(z + 8 - j, 8), 0), buf[8 - j])
         out = out + mm(choose(lax.rem(z + j, 8), 1), buf[j])
-        send_buf[j] = out.astype(BF16).reshape(4, 16, D)
-        y_send(lambda to: send_buf.at[j, to], recv_buf.at[y, j], ss, rs, j)
-
-    def y_single(n, block, ref, at, send_buf, recv_buf, ss, rs):
+        send_buf[j] = out.astype(BF16).reshape(4, 16, out.shape[1])
+        y_send(lambda to: send_buf.at[j, to], dst, ss, rs, j)
+
+    def y_single(n, block, ref, at, send_buf, dst, ss, rs):
         pick = jnp.concatenate([hot(ref, at, yy) for yy in range(4)], axis=0)
         out = mm(pick.astype(BF16)[:, :TOK], block)
+        w = out.shape[1] // 2
         for yy in range(4):
             rows = out[8 * yy : 8 * yy + 8]
-            send_buf[n, yy] = jnp.concatenate([rows[:, :1024], rows[:, 1024:]], axis=0).astype(BF16)
-        y_send(lambda to: send_buf.at[n, to], recv_buf.at[y, n], ss, rs, n)
-
-    def y_wait(recv_buf, rs, one_buf, one_rs):
+            send_buf[n, yy] = jnp.concatenate([rows[:, :w], rows[:, w:]], axis=0).astype(BF16)
+        y_send(lambda to: send_buf.at[n, to], dst, ss, rs, n)
+
+    def y_wait(view, rs, one_buf, one_rs, fill):
         for m in range(4):
             for j in range(1, 4):
-                drain(recv_buf.at[0, 0], rs.at[j, m])
+                drain(view, rs.at[j, m])
             for n in range(2):
                 drain(one_buf.at[0, 0], one_rs.at[n, m])
         for yy in range(4):
@@ -198,7 +207,7 @@
             for n in range(2):
                 a = one_buf[yy, n].astype(F32)
                 parts.append(jnp.concatenate([a[0:8], a[8:16]], axis=1))
-            recv_buf[yy, 0] = jnp.concatenate(parts, axis=0).astype(BF16)
+            fill(yy, jnp.concatenate(parts, axis=0).astype(BF16))
 
     def arrive(down, up, k):
         if k < len(down):
@@ -210,23 +219,45 @@
             if k + 1 < len(up):
                 up[k + 1].start()
 
-    y_single(0, tokens[...], zmsg, z, et, qt, es_t, er_t)
-    y_single(0, grads[...], zmsg, z, eg, qg, es_g, er_g)
-
-    drain(zin, rk_r)
-    own_z = zin.at[:, pl.ds(8, 8), :]
+    def cut(h):
+        return pl.ds(1024 * h, 1024)
+
+    def t_pair(j):
+        y_pair(j, zt, yt, rt.at[y, j], ys_t, yr_t)
+
+    def t_single(n, block, ref, at):
+        y_single(n, block, ref, at, et, qt.at[y, n], es_t, er_t)
+
+    def g_pair(h, j):
+        y_pair(j, zg.at[h], yg.at[h], rg.at[y, j, :, cut(h)], ys_g.at[h], yr_g.at[h])
+
+    def g_single(h, n, block, ref, at):
+        y_single(n, block, ref, at, eg.at[h], qg.at[h, y, n], es_g.at[h], er_g.at[h])
+
+    t_single(0, tokens[...], rk_out, z)
+    g_single(0, 0, grads[:, 0:1024], rk_out, z)
+    g_single(1, 0, grads[:, 1024:2048], rk_out, z)
+
+    drain(rk_in, rk_r)
+    drain(pk_in, pk_r)
     own_rows = lall.at[core, x, pl.ds(pl.multiple_of(y * 8, 8), 8)]
-    pltpu.make_async_copy(own_z, own_rows, lg_r).start()
+    pltpu.make_async_copy(pk_in, own_rows, lg_r).start()
+    pltpu.make_async_copy(rk_in.at[:, y], rk_col.at[y], rc_r).start()
     lg_copies = []
     for m in range(1, 4):
-        c = remote(
-            own_z, own_rows, lg_s.at[m - 1], lg_r, (me_d, lax.rem(y + m, 4) * 8 + z)
-        )
+        to = lax.rem(y + m, 4)
+        dev = (me_d, to * 8 + z)
+        lg_copies.append(remote(pk_in, own_rows, lg_s.at[m - 1], lg_r, dev))
+        lg_copies.append(remote(rk_in.at[:, to], rk_col.at[y], rc_s.at[m - 1], rc_r, dev))
+    for c in lg_copies:
         c.start()
-        lg_copies.append(c)
-
+
+    far = lax.rem(z + 4, 8)
     arrive(t_dn, t_up, 0)
-    y_pair(1, zt, yt, rt, ys_t, yr_t)
+    t_pair(1)
+    arrive(g_dn[0], g_up[0], 0)
+    g_pair(0, 1)
+    arrive(g_dn[1], g_up[1], 0)
     drain(lall.at[core, x], lg_r)
     others(
         NX,
@@ -234,22 +265,28 @@
             lall.at[core, x], lall.at[core, x], x_s, x_r, (lax.rem(x + k, NX) * 2 + core, me_e)
         ).start(),
     )
-    arrive(g_dn, g_up, 0)
-    y_pair(1, zg, yg, rg, ys_g, yr_g)
     arrive(t_dn, t_up, 1)
-    y_pair(2, zt, yt, rt, ys_t, yr_t)
-    arrive(g_dn, g_up, 1)
-    y_pair(2, zg, yg, rg, ys_g, yr_g)
+    t_pair(2)
+    arrive(g_dn[0], g_up[0], 1)
+    g_pair(0, 2)
+    arrive(g_dn[1], g_up[1], 1)
     arrive(t_dn, t_up, 2)
-    y_pair(3, zt, yt, rt, ys_t, yr_t)
+    t_pair(3)
+    arrive(g_dn[0], g_up[0], 2)
+    g_pair(0, 3)
+    arrive(g_dn[1], g_up[1], 2)
+    arrive(t_dn, t_up, 3)
+    t_single(1, zt[4], rk_in, far)
     drain(lall.at[core, pl.ds(0, NX - 1)], x_r)
     logit_pair = remote(lall.at[core], lall.at[core], p_s, p_r, partner)
     logit_pair.start()
-    arrive(g_dn, g_up, 2)
-    far = lax.rem(z + 4, 8)
-    arrive(t_dn, t_up, 3)
-    y_single(1, zt[4], zin, far, et, qt, es_t, er_t)
-    y_pair(3, zg, yg, rg, ys_g, yr_g)
+    arrive(g_dn[0], g_up[0], 3)
+    g_single(0, 1, zg[0, 4], rk_in, far)
+    g_pair(1, 1)
+    g_pair(1, 2)
+    g_pair(1, 3)
+    arrive(g_dn[1], g_up[1], 3)
+    g_single(1, 1, zg[1, 4], rk_in, far)
     drain(lall.at[1 - core], p_r)
 
     valid = iota((1024, 128), 1) < 96
@@ -281,8 +318,7 @@
             q_hi = q.astype(BF16)
             q_lo = (q - q_hi.astype(F32)).astype(BF16)
             d = q / (mm(q_hi, block_h) + mm(q_lo, block_h) + pad)
-            if p == 0:
-                dd[i] = d
+            dd[i] = d
             db[p, i] = d.astype(BF16)
             acc = acc + rows_of(d)
         c = total(acc)
@@ -291,12 +327,27 @@
     c3 = jnp.concatenate([cols[0:1, :], cols[8:9, :], cols[16:17, :]], axis=0)
     dens, quot = own_state(logits, c3)
     gates = NE * dens[3]
-    tile = jnp.zeros((8, 128), F32)
-    for slot in range(CAP):
-        one = jnp.sum(jnp.where(rank == slot, gates, 0.0), axis=0, keepdims=True)
-        tile = tile + jnp.where(sub8 == slot, jnp.broadcast_to(one, (8, 128)), 0.0)
-    eye8 = (iota((8, 128), 0) == lane8).astype(BF16)
-    gtile[...] = mm(tile.astype(BF16), eye8, TN)[0:NE].reshape(NE, 1, 128)
+
+    lane256, row256 = iota((256, 128), 1), iota((256, 128), 0)
+    q = dd[core, pl.ds(pl.multiple_of(x * 256, 256), 256), :] / c3[2:3, :]
+    q_hi = q.astype(BF16)
+    q_lo = (q - q_hi.astype(F32)).astype(BF16)
+    group = NE * q / (mm(q_hi, block_h) + mm(q_lo, block_h) + pad)
+    turned = jnp.zeros((256, 128), F32)
+    for n in range(3):
+        one = jnp.sum(jnp.where(lane256 == 32 * n + me_e, group, 0.0), axis=1, keepdims=True)
+        turned = turned + jnp.where(lane256 == 8 * n + lax.rem(row256, 8), one, 0.0)
+    gcol[...] = jnp.sum(turned.reshape(NE, 8, 128), axis=1).reshape(NE, 1, 128)
+    drain(rk_col, rc_r)
+    tiles = []
+    for yy in range(4):
+        for off in (0, 4, 7, 1, 6, 2, 5, 3):
+            zz = lax.rem(z + off, 8)
+            here = jnp.broadcast_to(rk_col[yy, zz], (8, 128)) == sub8.astype(F32)
+            tiles.append(jnp.where(here, jnp.broadcast_to(gcol[yy * 8 + zz], (8, 128)), 0.0))
+    gate = jnp.sum(jnp.concatenate(tiles, axis=0), axis=1, keepdims=True)
+    gate = gate.astype(BF16).astype(F32)
+
     def plane(src, dst, send, recv):
         pltpu.make_async_copy(src(me_e), dst, recv).start()
 
@@ -306,13 +357,13 @@
 
         others(NE, go)
 
-    plane(lambda e: gtile.at[e], gbuf.at[me_e], g_s, g_r)
-    arrive(g_dn, g_up, 3)
-    y_single(1, zg[4], zin, far, eg, qg, es_g, er_g)
-
     for c in loads:
         c.wait()
-    y_wait(rt, yr_t, qt, er_t)
+
+    def fill_t(yy, value):
+        rt[yy, 0] = value
+
+    y_wait(rt.at[0, 0], yr_t, qt, er_t, fill_t)
     cuts = []
     for o in range(4):
         at = pl.ds(pl.multiple_of(512 * o + 256 * (1 - core), 256), 256)
@@ -346,20 +397,61 @@
         zz = lax.rem(z + h * (j + 4 * ((4 - j) // 4)) + (1 - h) * (8 - j), 8)
         return yy * 8 + o, yy * 8 + zz
 
-    drain(gbuf, g_r)
-    tiles = []
-    for yy in range(4):
-        for off in (0, 4, 7, 1, 6, 2, 5, 3):
-            one = gbuf[yy * 8 + lax.rem(z + off, 8)]
-            tiles.append(jnp.where(lane8 == sub8, jnp.broadcast_to(one, (8, 128)), 0.0))
-    gate = jnp.sum(jnp.concatenate(tiles, axis=0), axis=1, keepdims=True)
-
-    y_wait(rg, yr_g, qg, er_g)
-    for b in range(4):
-        at = slice(512 * b, 512 * b + 512)
-        ds[:, at] = (gate * rg[:, :, :, at].reshape(256, 512).astype(F32)).astype(BF16)
-    ds_copy = remote(ds, pds, q_s.at[5], q_r.at[5], partner)
-    ds_copy.start()
+    def fill_g(h):
+        def f(yy, value):
+            rg[yy, 0, :, 1024 * h : 1024 * h + 1024] = value
+        return f
+
+    ds_copies = []
+
+    def scaled(h):
+        y_wait(rg.at[0, 0, :, cut(h)], yr_g.at[h], qg.at[h], er_g.at[h], fill_g(h))
+        for b in range(2 * h, 2 * h + 2):
+            at = slice(512 * b, 512 * b + 512)
+            ds[:, at] = (gate * rg[:, :, :, at].reshape(256, 512).astype(F32)).astype(BF16)
+        c = remote(ds.at[:, cut(h)], pds.at[:, cut(h)], q_s.at[5 + h], q_r.at[5 + h], partner)
+        c.start()
+        ds_copies.append(c)
+
+    def my_rows(ref, j):
+        o = lax.rem(x + j, NX)
+        return ref[pl.ds(pl.multiple_of(192 * o + 96 * core, 32), 96), :]
+
+    half, early = [], []
+
+    def down_half(h):
+        ds_copies[h].wait_recv()
+
+        def one(i, carry):
+            at = pl.ds(pl.multiple_of(1024 * h + i * 512, 512), 512)
+            to = pl.ds(pl.multiple_of(i * 512, 512), 512)
+            mine = jnp.concatenate([my_rows(ht, j) for j in range(4)], axis=0)
+            theirs = jnp.concatenate([my_rows(pht, j) for j in range(4)], axis=0)
+            out = mm(mine, ds[:, at]) + mm(theirs, pds[:, at])
+            for j in range(4):
+                g2[h, j, :, to] = out[96 * j : 96 * j + 96].astype(BF16)
+            return carry
+
+        lax.fori_loop(0, 2, one, 0)
+        top, low = pl.ds(0, 48), pl.ds(48, 48)
+        n = 2 * h
+        half.append(remote(g2.at[h, 2, top], ra2.at[h], h_s.at[n], h_r.at[n], right))
+        half.append(remote(g2.at[h, 2, low], rb2.at[h], h_s.at[n + 1], h_r.at[n + 1], left))
+        early.append(
+            remote(g2.at[h, 1, low], rc2.at[h, low], n_s.at[n], n_r.at[n], right)
+        )
+        early.append(
+            remote(g2.at[h, 3, top], rd2.at[h, top], n_s.at[n + 1], n_r.at[n + 1], left)
+        )
+        half[-2].start()
+        half[-1].start()
+
+    scaled(0)
+    ht_copy.wait_recv()
+    down_half(0)
+    early[0].start()
+    early[1].start()
+    scaled(1)
 
     def backward(i, total_score):
         at = pl.ds(pl.multiple_of(i * 256, 256), 256)
@@ -374,7 +466,7 @@
         return total_score + jnp.sum(h * hid[:, at], axis=1, keepdims=True)
 
     score = lax.fori_loop(0, 3, backward, jnp.zeros((256, 1), F32))
-    pair_copy = remote(pair, ppair, q_s.at[6], q_r.at[6], partner)
+    pair_copy = remote(pair, ppair, q_s.at[7], q_r.at[7], partner)
     pair_copy.start()
     spread8 = jnp.broadcast_to(score.astype(BF16).astype(F32), (256, 128)).reshape(NE, 8, 128)
     diag = iota((NE, 8, 128), 1) == iota((NE, 8, 128), 2)
@@ -387,38 +479,16 @@
 
     others(NE, send_score)
 
-    ht_copy.wait_recv()
-    ds_copy.wait_recv()
-
-    def my_rows(ref, j):
-        o = lax.rem(x + j, NX)
-        return ref[pl.ds(pl.multiple_of(192 * o + 96 * core, 32), 96), :]
-
-    def down_part(i, carry):
-        at = pl.ds(pl.multiple_of(i * 512, 512), 512)
-        mine = jnp.concatenate([my_rows(ht, j) for j in range(4)], axis=0)
-        theirs = jnp.concatenate([my_rows(pht, j) for j in range(4)], axis=0)
-        out = mm(mine, ds[:, at]) + mm(theirs, pds[:, at])
-        for j in range(4):
-            g2[j, :, at] = out[96 * j : 96 * j + 96].astype(BF16)
-        return carry
-
-    lax.fori_loop(0, 4, down_part, 0)
-    half = [
-        remote(g2.at[2, pl.ds(0, 48)], ra2, h_s.at[0], h_r.at[0], right),
-        remote(g2.at[2, pl.ds(48, 48)], rb2, h_s.at[1], h_r.at[1], left),
-    ]
+    down_half(1)
     for n in range(2):
         at = pl.ds(64 * n, 64)
         half += [
-            remote(g1.at[2, at], ra1.at[at], h_s.at[2 * n + 2], h_r.at[2 * n + 2], right),
+            remote(g1.at[2, at], ra1.at[at], h_s.at[2 * n + 4], h_r.at[2 * n + 4], right),
             remote(
                 g1.at[2, pl.ds(128 + 64 * n, 64)], rb1.at[at],
-                h_s.at[2 * n + 3], h_r.at[2 * n + 3], left,
+                h_s.at[2 * n + 5], h_r.at[2 * n + 5], left,
             ),
         ]
-    half[0].start()
-    half[1].start()
     for c in cuts:
         c.wait_recv()
     pair_copy.wait_recv()
@@ -437,8 +507,8 @@
         lax.fori_loop(0, 3, one, 0)
 
     pair_part(2)
-    half[2].start()
-    half[3].start()
+    for c in half[4:8]:
+        c.start()
     for b in range(4):
         at = slice(512 * b, 512 * b + 512)
         out = mm(gg[...], wg[at, :], NT) + mm(ug[...], wu[at, :], NT)
@@ -497,19 +567,13 @@
             btile, bbuf.at[me_d], b_s, b_r, (lax.rem(me_d + k, ND), me_e)
         ).start(),
     )
-    half[4].start()
-    half[5].start()
-    early = [
-        remote(g2.at[1, pl.ds(48, 48)], rc2.at[pl.ds(48, 48)], n_s.at[0], n_r.at[0], right),
-        remote(g2.at[3, pl.ds(0, 48)], rd2.at[pl.ds(0, 48)], n_s.at[1], n_r.at[1], left),
-    ]
     for n in range(2):
         up, down = pl.ds(128 + 64 * n, 64), pl.ds(64 * n, 64)
         early += [
-            remote(g1.at[1, up], rc1.at[up], n_s.at[2 * n + 2], n_r.at[2 * n + 2], right),
-            remote(g1.at[3, down], rd1.at[down], n_s.at[2 * n + 3], n_r.at[2 * n + 3], left),
+            remote(g1.at[1, up], rc1.at[up], n_s.at[2 * n + 4], n_r.at[2 * n + 4], right),
+            remote(g1.at[3, down], rd1.at[down], n_s.at[2 * n + 5], n_r.at[2 * n + 5], left),
         ]
-    for c in early[0:4]:
+    for c in early[2:6]:
         c.start()
 
     drain(bbuf, b_r)
@@ -548,16 +612,29 @@
 
     for c in half:
         c.wait_recv()
-    add_rows(48, 48, [take(g2, 1, 0), lambda at: ra2[at, :]], put(g2, 1, 0))
-    add_rows(48, 48, [take(g2, 3, 48), lambda at: rb2[at, :]], put(g2, 3, 48))
+    for h in range(2):
+        add_rows(
+            48, 48, [take(g2.at[h], 1, 0), lambda at, h=h: ra2[h, at, :]], put(g2.at[h], 1, 0)
+        )
+        add_rows(
+            48, 48, [take(g2.at[h], 3, 48), lambda at, h=h: rb2[h, at, :]], put(g2.at[h], 3, 48)
+        )
     add_rows(128, 32, [take(g1, 1, 0), lambda at: ra1[at, :]], put(g1, 1, 0))
     add_rows(128, 32, [take(g1, 3, 128), lambda at: rb1[at, :]], put(g1, 3, 128))
-    late = [
-        remote(g2.at[1, pl.ds(0, 48)], rc2.at[pl.ds(0, 48)], m_s.at[0], m_r.at[0], right),
-        remote(g2.at[3, pl.ds(48, 48)], rd2.at[pl.ds(48, 48)], m_s.at[1], m_r.at[1], left),
-        remote(g1.at[1, pl.ds(0, 128)], rc1.at[pl.ds(0, 128)], m_s.at[2], m_r.at[2], right),
-        remote(g1.at[3, pl.ds(128, 128)], rd1.at[pl.ds(128, 128)], m_s.at[3], m_r.at[3], left),
+    late = []
+    for h in range(2):
+        top, low = pl.ds(0, 48), pl.ds(48, 48)
+        late += [
+            remote(g2.at[h, 1, top], rc2.at[h, top], m_s.at[2 * h], m_r.at[2 * h], right),
+            remote(
+                g2.at[h, 3, low], rd2.at[h, low], m_s.at[2 * h + 1], m_r.at[2 * h + 1], left
+            ),
+        ]
+    late += [
+        remote(g1.at[1, pl.ds(0, 128)], rc1.at[pl.ds(0, 128)], m_s.at[4], m_r.at[4], right),
+        remote(g1.at[3, pl.ds(128, 128)], rd1.at[pl.ds(128, 128)], m_s.at[5], m_r.at[5], left),
     ]
+
     drain(rrecv, rs_r)
     dsum[...] = jnp.sum(rrecv[...].astype(F32), axis=0).astype(BF16)
     pltpu.make_async_copy(dsum, drecv.at[me_d], d_r).start()
@@ -567,8 +644,8 @@
             dsum, drecv.at[me_d], d_s, d_r, (lax.rem(me_d + k, ND), me_e)
         ).start(),
     )
-    early[4].start()
-    early[5].start()
+    early[6].start()
+    early[7].start()
     for c in late:
         c.start()
     drain(drecv, d_r)
@@ -588,21 +665,33 @@
             ref[at, :] = value.astype(BF16)
         return f
 
-    add_rows(
-        96, 48, [take(g2, 0, 0), lambda at: rc2[at, :], lambda at: rd2[at, :]], store(down_out)
-    )
+    def store_half(h):
+        def f(at, value):
+            down_out[at, 1024 * h : 1024 * h + 1024] = value.astype(BF16)
+        return f
+
+    for h in range(2):
+        add_rows(
+            96, 48,
+            [
+                take(g2.at[h], 0, 0),
+                lambda at, h=h: rc2[h, at, :],
+                lambda at, h=h: rd2[h, at, :],
+            ],
+            store_half(h),
+        )
     add_rows(
         256, 32, [take(g1, 0, 0), lambda at: rc1[at, :], lambda at: rd1[at, :]], store(pair_out)
     )
     drain(router_out, o_r)
 
-    for c in t_dn + t_up + g_dn + g_up + y_copies + lg_copies + cuts + half + early + late:
+    for c in t_dn + t_up + g_dn[0] + g_dn[1] + g_up[0] + g_up[1] + ds_copies + y_copies + lg_copies + cuts + half + early + late:
         c.wait_send()
-    for c in (logit_pair, ht_copy, ds_copy, pair_copy):
+    for c in (logit_pair, ht_copy, pair_copy):
         c.wait_send()
-    drain(zin.at[pl.ds(0, 7)], rk_s)
+    drain(rk_in.at[pl.ds(0, 7)], rk_s)
+    drain(pk_in.at[pl.ds(0, 7)], pk_s)
     drain(lall.at[0, pl.ds(0, NX - 1)], x_s)
-    drain(gbuf.at[pl.ds(0, NE - 1)], g_s)
     drain(ret.at[pl.ds(0, NE - 1)], ret_s)
     drain(sbuf.at[pl.ds(0, NE - 1)], sc_s)
     drain(abuf.at[pl.ds(0, NE - 1)], a_s)
@@ -629,13 +718,14 @@
         out_specs=(VM,) * 4,
         scratch_shapes=[
             V((D, FF), BF16), V((D, FF), BF16), V((FF, D), BF16),
-            V((8, 16, 128), F32), V((8, 16, 128), F32),
-            V((2, 4, 16, 1024), BF16), V((2, 4, 16, 1024), BF16),
-            V((4, 2, 16, 1024), BF16), V((4, 2, 16, 1024), BF16),
+            V((8, 4, 1, 128), F32), V((8, 4, 1, 128), F32), V((4, 8, 1, 128), F32),
+            V((8, 128), F32), V((8, 8, 128), F32),
+            V((2, 4, 16, 1024), BF16), V((2, 2, 4, 16, 512), BF16),
+            V((4, 2, 16, 1024), BF16), V((2, 4, 2, 16, 512), BF16),
             V((2, NX, NE, 8, 128), F32), V((2, 1024, 128), F32), V((2, 2, 1024, 128), BF16),
-            V((24, 128), F32), V((2, 128, 128), F32), V((NE, 1, 128), F32), V((NE, 1, 128), F32),
-            V((8, TOK, D), BF16), V((8, TOK, D), BF16),
-            V((4, 4, 16, D), BF16), V((4, 4, 16, D), BF16),
+            V((24, 128), F32), V((2, 128, 128), F32), V((NE, 1, 128), F32),
+            V((8, TOK, D), BF16), V((2, 8, TOK, 1024), BF16),
+            V((4, 4, 16, D), BF16), V((2, 4, 4, 16, 1024), BF16),
             V((4, 4, 16, D), BF16), V((4, 4, 16, D), BF16),
             V((4, 4, 4, 16, 256), BF16),
             V((256, FF), F32), V((256, FF), F32), V((256, FF), F32),
@@ -643,11 +733,11 @@
             V((256, D), BF16), V((256, D), BF16),
             V((256, FF), BF16), V((256, FF), BF16),
             V((256, 2 * FF), BF16), V((256, 2 * FF), BF16),
-            V((4, 256, 2 * FF), BF16), V((4, 96, D), BF16),
-            V((128, 2 * FF), BF16), V((48, D), BF16),
-            V((128, 2 * FF), BF16), V((48, D), BF16),
-            V((256, 2 * FF), BF16), V((96, D), BF16),
-            V((256, 2 * FF), BF16), V((96, D), BF16),
+            V((4, 256, 2 * FF), BF16), V((2, 4, 96, 1024), BF16),
+            V((128, 2 * FF), BF16), V((2, 48, 1024), BF16),
+            V((128, 2 * FF), BF16), V((2, 48, 1024), BF16),
+            V((256, 2 * FF), BF16), V((2, 96, 1024), BF16),
+            V((256, 2 * FF), BF16), V((2, 96, 1024), BF16),
             V((NE, 16, 1024), BF16), V((NE, 16, 1024), BF16),
             V((NE, 1, 128), F32), V((NE, 1, 128), F32),
             V((1, 128), F32), V((NE, 1, 128), F32),
@@ -655,13 +745,14 @@
             V((NE, 16, 128), BF16), V((NE, 16, 128), BF16),
             V((16, 128), BF16), V((ND, 16, 128), BF16), V((16, 128), BF16),
             dma((3,)),
-            dma((8,)), dma((8,)), dma((8,)), dma((8,)),
-            dma((4, 4)), dma((4, 4)), dma((4, 4)), dma((4, 4)),
-            dma((2, 4)), dma((2, 4)), dma((2, 4)), dma((2, 4)),
-            dma((7,)), dma((7,)),
-            dma((6,)), dma((6,)), dma((6,)), dma((6,)), dma((4,)), dma((4,)), dma((3,)),
+            dma((8,)), dma((8,)), dma((2, 8)), dma((2, 8)),
+            dma((4, 4)), dma((4, 4)), dma((2, 4, 4)), dma((2, 4, 4)),
+            dma((2, 4)), dma((2, 4)), dma((2, 2, 4)), dma((2, 2, 4)),
+            dma((8,)), dma((8,)),
+            dma((8,)), dma((8,)), dma((8,)), dma((8,)), dma((6,)), dma((6,)),
+            dma((3,)), dma, dma((3,)), dma,
         ]
-        + [dma] * 23,
+        + [dma] * 22,
         compiler_params=pltpu.CompilerParams(
             collective_id=0, has_side_effects=True, vmem_limit_bytes=52 * 1024 * 1024
         ),

time: 95.5 us -> 94.6 us (level)
  Pallas kernels: 91.3 us -> 90 us
    pallas_call x1, Pallas kernels: 90 us -> 88.8 us  [moe(): pl.pallas_call(moe_kernel, name='moe', out_shape=(jax.ShapeDtypeStruct((T...]
where the time goes in v4:
time: 94.6 us; the launch traced here: 94 us
  Pallas kernels  90 us (95%)
  local copies, waits for them, and re-layouts  3.37 us (4%)
    pallas_call x1, Pallas kernels, moe(): pl.pallas_call(moe_kernel, name='moe', out_shape=(jax.ShapeDtypeStruct((T...  88.8 us
    unnamed x8, local copies, waits for them, and re-layouts  3.37 us

profile of v4, /device:TPU:1, one launch (start us, length us, event | category | flops | bytes accessed | tf_op | source)
XLA Modules:
  0.0 94.0 jit_solution(1422775211029186640)
XLA Ops:
  0.6 0.0 copy-start
  0.6 0.9 copy-done
  1.5 0.0 copy-start.1
  1.5 0.9 copy-done.1
  2.4 0.0 copy-start.2
  2.4 0.9 copy-done.2
  3.3 0.0 copy-start.3
  3.3 0.7 copy-done.3
  4.0 88.8 %moe.1 = (bf16[24,2048]{1,0:T(8,128)(2,1)S(1)}, bf16[256,1536]{1,0:T(8,128)(2,1)S(1)}, bf16[96,2048]{1,0:T(8,128)(2,1)S(1)}, bf16[32,16,128]{2,1,0:T(8,128)(2,1)S(1)}) custom-call(bf16[24,2048]{1,0:T(8,128)(2,1)S(1)} %copy-done.1, bf16[24,2048]{1,0:T(8,128)(2,1)S(1)} %copy-done.2, s32[8,24]{1,0:T(8,128)S(1)} %bitcast.4, bf16[32,2048]{1,0:T(8,128)(2,1)S(1)} %bitcast.3, ...), custom_call_target="tpu_custom_call" | custom-call | tf_op jit(solution)/shard_map/moe/pallas_call | solution.py:708
  92.8 1.2 %write.1 = (bf16[24,2048]{1,0:T(8,128)(2,1)}, f32[32,2048]{1,0:T(8,128)}, bf16[1,256,768]{2,1,0:T(8,128)(2,1)}, bf16[1,256,768]{2,1,0:T(8,128)(2,1)}, bf16[1,96,2048]{2,1,0:T(8,128)(2,1)}) custom-call(bf16[24,2048]{1,0:T(8,128)(2,1)S(1)} %get-tuple-element.14.gt, bf16[256,1536]{1,0:T(8,128)(2,1)S(1)} %get-tuple-element.15.pair, ...), custom_call_target="tpu_custom_call" | custom-call | tf_op jit(solution)/shard_map/write/pallas_call | solution.py:773
Async XLA Ops:
  0.6 0.9 copy-start
  1.5 0.9 copy-start.1
  2.4 0.9 copy-start.2
  3.3 0.7 copy-start.3

commit v5 on v4

--- a/solution.py
+++ b/solution.py
@@ -68,19 +68,27 @@
 
 
 def moe_kernel(
-    tokens, grads, ids, rw, wg_hbm, wu_hbm, wd_hbm,
+    tokens_hbm, grads_hbm, ids_hbm, rw_hbm, wg_hbm, wu_hbm, wd_hbm,
     gt_out, pair_out, down_out, router_out,
-    wg, wu, wd, rk_out, rk_in, rk_col, pk_out, pk_in, et, eg, qt, qg,
+    tokens, grads, ids, rw, wg, wu, wd, rk_out, rk_in, rk_col, pk_out, pk_in, et, eg, qt, qg,
     lall, dd, db, cols, gram, gcol,
     zt, zg, yt, yg, rt, rg, pt, hid, act, dsl, ht, pht, ds, pds, gg, ug, pair, ppair,
     g1, g2, ra1, ra2, rb1, rb2, rc1, rc2, rd1, rd2,
     bsend, ret, stile, sbuf, atile, abuf, btile, bbuf, rsend, rrecv, dsum, drecv, fin,
-    w_sem, zs_t, zr_t, zs_g, zr_g, ys_t, yr_t, ys_g, yr_g, es_t, er_t, es_g, er_g, q_s, q_r, h_s, h_r, n_s, n_r, m_s, m_r,
-    lg_s, lg_r, rc_s, rc_r, rk_s, rk_r, pk_s, pk_r, x_s, x_r, p_s, p_r, ret_s, ret_r, sc_s, sc_r,
+    in_sem, w_sem, zs_t, zr_t, zs_g, zr_g, ys_t, yr_t, ys_g, yr_g, es_t, er_t, es_g, er_g, q_s, q_r, h_s, h_r, n_s, n_r, m_s, m_r,
+    ht_s, ht_r, lg_s, lg_r, rc_s, rc_r, rk_s, rk_r, pk_s, pk_r, x_s, x_r, p_s, p_r, ret_s, ret_r, sc_s, sc_r,
     a_s, a_r, b_s, b_r, rs_s, rs_r, d_s, d_r, o_s, o_r,
 ):
     me_d, me_e, x, core = place()
     y, z = me_e // 8, lax.rem(me_e, 8)
+    inputs = [
+        pltpu.make_async_copy(a, b, in_sem.at[n])
+        for n, (a, b) in enumerate(
+            ((tokens_hbm, tokens), (grads_hbm, grads), (ids_hbm, ids), (rw_hbm, rw))
+        )
+    ]
+    for c in inputs:
+        c.start()
     barrier = pltpu.get_barrier_semaphore()
     others(
         NE,
@@ -100,6 +108,8 @@
     ]
     for c in loads:
         c.start()
+    for c in inputs:
+        c.wait()
     partner = (x * 2 + 1 - core, me_e)
     right = (lax.rem(x + 1, NX) * 2 + core, me_e)
     left = (lax.rem(x + 3, NX) * 2 + core, me_e)
@@ -386,9 +396,10 @@
         ht[at, :] = h.T.astype(BF16)
         return carry
 
-    lax.fori_loop(0, 3, forward, 0)
-    ht_copy = remote(ht, pht, q_s.at[4], q_r.at[4], partner)
-    ht_copy.start()
+    ht_copies = [
+        remote(ht.at[r], pht.at[r], ht_s.at[n], ht_r.at[n], partner)
+        for n, r in enumerate(pl.ds(256 * i, 256) for i in range(3))
+    ]
 
     def where_from(k):
         o = lax.rem(k, 8)
@@ -422,17 +433,19 @@
     def down_half(h):
         ds_copies[h].wait_recv()
 
-        def one(i, carry):
-            at = pl.ds(pl.multiple_of(1024 * h + i * 512, 512), 512)
-            to = pl.ds(pl.multiple_of(i * 512, 512), 512)
-            mine = jnp.concatenate([my_rows(ht, j) for j in range(4)], axis=0)
-            theirs = jnp.concatenate([my_rows(pht, j) for j in range(4)], axis=0)
-            out = mm(mine, ds[:, at]) + mm(theirs, pds[:, at])
-            for j in range(4):
-                g2[h, j, :, to] = out[96 * j : 96 * j + 96].astype(BF16)
-            return carry
-
-        lax.fori_loop(0, 2, one, 0)
+        def rows(js):
+            def one(i, carry):
+                at = pl.ds(pl.multiple_of(1024 * h + i * 512, 512), 512)
+                to = pl.ds(pl.multiple_of(i * 512, 512), 512)
+                mine = jnp.concatenate([my_rows(ht, j) for j in js], axis=0)
+                theirs = jnp.concatenate([my_rows(pht, j) for j in js], axis=0)
+                out = mm(mine, ds[:, at]) + mm(theirs, pds[:, at])
+                for n, j in enumerate(js):
+                    g2[h, j, :, to] = out[96 * n : 96 * n + 96].astype(BF16)
+                return carry
+
+            lax.fori_loop(0, 2, one, 0)
+
         top, low = pl.ds(0, 48), pl.ds(48, 48)
         n = 2 * h
         half.append(remote(g2.at[h, 2, top], ra2.at[h], h_s.at[n], h_r.at[n], right))
@@ -443,11 +456,18 @@
         early.append(
             remote(g2.at[h, 3, top], rd2.at[h, top], n_s.at[n + 1], n_r.at[n + 1], left)
         )
+        rows((2,))
         half[-2].start()
         half[-1].start()
-
-    scaled(0)
-    ht_copy.wait_recv()
+        rows((1, 3, 0))
+
+    for n in range(3):
+        lax.fori_loop(n, n + 1, forward, 0)
+        ht_copies[n].start()
+        if n == 1:
+            scaled(0)
+    for c in ht_copies:
+        c.wait_recv()
     down_half(0)
     early[0].start()
     early[1].start()
@@ -635,6 +655,8 @@
         remote(g1.at[3, pl.ds(128, 128)], rd1.at[pl.ds(128, 128)], m_s.at[5], m_r.at[5], left),
     ]
 
+    for c in late[0:2] + early[6:8]:
+        c.start()
     drain(rrecv, rs_r)
     dsum[...] = jnp.sum(rrecv[...].astype(F32), axis=0).astype(BF16)
     pltpu.make_async_copy(dsum, drecv.at[me_d], d_r).start()
@@ -644,9 +666,7 @@
             dsum, drecv.at[me_d], d_s, d_r, (lax.rem(me_d + k, ND), me_e)
         ).start(),
     )
-    early[6].start()
-    early[7].start()
-    for c in late:
+    for c in late[2:6]:
         c.start()
     drain(drecv, d_r)
     fin[...] = jnp.sum(drecv[...].astype(F32), axis=0).astype(BF16)
@@ -687,7 +707,7 @@
 
     for c in t_dn + t_up + g_dn[0] + g_dn[1] + g_up[0] + g_up[1] + ds_copies + y_copies + lg_copies + cuts + half + early + late:
         c.wait_send()
-    for c in (logit_pair, ht_copy, pair_copy):
+    for c in [logit_pair, pair_copy] + ht_copies:
         c.wait_send()
     drain(rk_in.at[pl.ds(0, 7)], rk_s)
     drain(pk_in.at[pl.ds(0, 7)], pk_s)
@@ -714,9 +734,10 @@
             jax.ShapeDtypeStruct((96, D), BF16),
             jax.ShapeDtypeStruct((NE, 16, 128), BF16),
         ),
-        in_specs=[VM] * 4 + [hbm] * 3,
+        in_specs=[hbm] * 7,
         out_specs=(VM,) * 4,
         scratch_shapes=[
+            V((TOK, D), BF16), V((TOK, D), BF16), V((8, TOK), jnp.int32), V((NE, D), BF16),
             V((D, FF), BF16), V((D, FF), BF16), V((FF, D), BF16),
             V((8, 4, 1, 128), F32), V((8, 4, 1, 128), F32), V((4, 8, 1, 128), F32),
             V((8, 128), F32), V((8, 8, 128), F32),
@@ -744,13 +765,13 @@
             V((1, 128), F32), V((ND, 1, 128), F32),
             V((NE, 16, 128), BF16), V((NE, 16, 128), BF16),
             V((16, 128), BF16), V((ND, 16, 128), BF16), V((16, 128), BF16),
-            dma((3,)),
+            dma((4,)), dma((3,)),
             dma((8,)), dma((8,)), dma((2, 8)), dma((2, 8)),
             dma((4, 4)), dma((4, 4)), dma((2, 4, 4)), dma((2, 4, 4)),
             dma((2, 4)), dma((2, 4)), dma((2, 2, 4)), dma((2, 2, 4)),
             dma((8,)), dma((8,)),
             dma((8,)), dma((8,)), dma((8,)), dma((8,)), dma((6,)), dma((6,)),
-            dma((3,)), dma, dma((3,)), dma,
+            dma((3,)), dma((3,)), dma((3,)), dma, dma((3,)), dma,
         ]
         + [dma] * 22,
         compiler_params=pltpu.CompilerParams(
@@ -788,7 +809,11 @@
 
 def per_device(tokens, out_grad, expert_ids, router_weight, w_gate, w_up, w_down):
     gt, pair, down, router = moe(
-        tokens, out_grad, expert_ids.T, router_weight.T, w_gate, w_up, w_down
+        *[
+            pltpu.with_memory_space_constraint(a, pltpu.HBM)
+            for a in (tokens, out_grad, expert_ids.T, router_weight.T)
+        ],
+        w_gate, w_up, w_down
     )
     gt, router, gate, up, down = write(gt, pair, down, router)
     return gt, router.T, gate, up, down

time: 94.6 us -> 87.2 us (0.922)
  Pallas kernels: 90 us -> 86.5 us
  local copies, waits for them, and re-layouts: 3.37 us -> 0 us
    pallas_call x1, Pallas kernels: 88.8 us -> 85.3 us  [moe(): pl.pallas_call(moe_kernel, name='moe', out_shape=(jax.ShapeDtypeStruct((T...]
    unnamed x8 -> x0, local copies, waits for them, and re-layouts: 3.37 us -> none
where the time goes in v5:
time: 87.2 us
  Pallas kernels  86.5 us (99%)
    pallas_call x1, Pallas kernels, moe(): pl.pallas_call(moe_kernel, name='moe', out_shape=(jax.ShapeDtypeStruct((T...  85.3 us

profile of v5, /device:TPU:1, one launch (start us, length us, event | category | flops | bytes accessed | tf_op | source)
XLA Modules:
  0.0 87.2 jit_solution(5261953186617079687)
XLA Ops:
  0.6 85.3 %moe.1 = (bf16[24,2048]{1,0:T(8,128)(2,1)S(1)}, bf16[256,1536]{1,0:T(8,128)(2,1)S(1)}, bf16[96,2048]{1,0:T(8,128)(2,1)S(1)}, bf16[32,16,128]{2,1,0:T(8,128)(2,1)S(1)}) custom-call(bf16[24,2048]{1,0:T(8,128)(2,1)} %tokens_hbm.1, bf16[24,2048]{1,0:T(8,128)(2,1)} %grads_hbm.1, s32[8,24]{1,0:T(8,128)} %bitcast.4, bf16[32,2048]{1,0:T(8,128)(2,1)} %bitcast.3, ...), custom_call_target="tpu_custom_call" | custom-call | tf_op jit(solution)/shard_map/moe/pallas_call | solution.py:728
  85.9 1.2 %write.1 = (bf16[24,2048]{1,0:T(8,128)(2,1)}, f32[32,2048]{1,0:T(8,128)}, bf16[1,256,768]{2,1,0:T(8,128)(2,1)}, bf16[1,256,768]{2,1,0:T(8,128)(2,1)}, bf16[1,96,2048]{2,1,0:T(8,128)(2,1)}) custom-call(bf16[24,2048]{1,0:T(8,128)(2,1)S(1)} %get-tuple-element.14.gt, bf16[256,1536]{1,0:T(8,128)(2,1)S(1)} %get-tuple-element.15.pair, ...), custom_call_target="tpu_custom_call" | custom-call | tf_op jit(solution)/shard_map/write/pallas_call | solution.py:794

commit v6 on v5

--- a/solution.py
+++ b/solution.py
@@ -155,18 +155,18 @@
             z_down if sign > 0 else z_up,
         )
 
-    t_dn = [z_copy(tokens, zt, zs_t, zr_t, k, -1) for k in (1, 2, 3, 4)]
-    t_up = [z_copy(tokens, zt, zs_t, zr_t, k, 1) for k in (1, 2, 3)]
-    g_dn, g_up = [], []
-    for h in range(2):
-        own = grads.at[:, pl.ds(1024 * h, 1024)]
-        g_dn.append(
-            [z_copy(own, zg.at[h], zs_g.at[h], zr_g.at[h], k, -1) for k in (1, 2, 3)]
-        )
-        g_up.append(
-            [z_copy(own, zg.at[h], zs_g.at[h], zr_g.at[h], k, 1) for k in (1, 2, 3, 4)]
-        )
-    for pipe in (t_dn, t_up, g_dn[0], g_up[0], g_dn[1], g_up[1]):
+    def pipes(ref, buf, ss, rs, down, up):
+        dn_list, up_list = [], []
+        for h in range(2):
+            own = ref.at[:, pl.ds(1024 * h, 1024)]
+            args = (own, buf.at[h], ss.at[h], rs.at[h])
+            dn_list.append([z_copy(*args, k, -1) for k in range(1, down + 1)])
+            up_list.append([z_copy(*args, k, 1) for k in range(1, up + 1)])
+        return dn_list, up_list
+
+    t_dn, t_up = pipes(tokens, zt, zs_t, zr_t, 4, 3)
+    g_dn, g_up = pipes(grads, zg, zs_g, zr_g, 3, 4)
+    for pipe in (t_dn[0], t_up[0], t_dn[1], t_up[1], g_dn[0], g_up[0]):
         pipe[0].start()
 
     def hot(ref, at, yy):
@@ -192,8 +192,8 @@
         pltpu.make_async_copy(src(y), dst, rs.at[j, 0]).start()
 
     def y_pair(j, buf, send_buf, dst, ss, rs):
-        out = mm(choose(lax.rem(z + 8 - j, 8), 0), buf[8 - j])
-        out = out + mm(choose(lax.rem(z + j, 8), 1), buf[j])
+        out = mm(choose(lax.rem(z + 8 - j, 8), 0), buf(8 - j))
+        out = out + mm(choose(lax.rem(z + j, 8), 1), buf(j))
         send_buf[j] = out.astype(BF16).reshape(4, 16, out.shape[1])
         y_send(lambda to: send_buf.at[j, to], dst, ss, rs, j)
 
@@ -232,21 +232,23 @@
     def cut(h):
         return pl.ds(1024 * h, 1024)
 
+    def t_block(n):
+        return jnp.concatenate([zt[0, n], zt[1, n]], axis=1)
+
     def t_pair(j):
-        y_pair(j, zt, yt, rt.at[y, j], ys_t, yr_t)
+        y_pair(j, t_block, yt, rt.at[y, j], ys_t, yr_t)
 
     def t_single(n, block, ref, at):
         y_single(n, block, ref, at, et, qt.at[y, n], es_t, er_t)
 
     def g_pair(h, j):
-        y_pair(j, zg.at[h], yg.at[h], rg.at[y, j, :, cut(h)], ys_g.at[h], yr_g.at[h])
+        y_pair(j, lambda n: zg[h, n], yg.at[h], rg.at[y, j, :, cut(h)], ys_g.at[h], yr_g.at[h])
 
     def g_single(h, n, block, ref, at):
         y_single(n, block, ref, at, eg.at[h], qg.at[h, y, n], es_g.at[h], er_g.at[h])
 
     t_single(0, tokens[...], rk_out, z)
     g_single(0, 0, grads[:, 0:1024], rk_out, z)
-    g_single(1, 0, grads[:, 1024:2048], rk_out, z)
 
     drain(rk_in, rk_r)
     drain(pk_in, pk_r)
@@ -263,11 +265,19 @@
         c.start()
 
     far = lax.rem(z + 4, 8)
-    arrive(t_dn, t_up, 0)
+    def arrive_t(k):
+        for h in range(2):
+            arrive(t_dn[h], t_up[h], k)
+
+    def arrive_g(h, k):
+        arrive(g_dn[h], g_up[h], k)
+
+    arrive_t(0)
     t_pair(1)
-    arrive(g_dn[0], g_up[0], 0)
+    arrive_g(0, 0)
+    g_dn[1][0].start()
+    g_up[1][0].start()
     g_pair(0, 1)
-    arrive(g_dn[1], g_up[1], 0)
     drain(lall.at[core, x], lg_r)
     others(
         NX,
@@ -275,28 +285,28 @@
             lall.at[core, x], lall.at[core, x], x_s, x_r, (lax.rem(x + k, NX) * 2 + core, me_e)
         ).start(),
     )
-    arrive(t_dn, t_up, 1)
+    arrive_t(1)
     t_pair(2)
-    arrive(g_dn[0], g_up[0], 1)
+    arrive_g(0, 1)
+    arrive_g(1, 0)
     g_pair(0, 2)
-    arrive(g_dn[1], g_up[1], 1)
-    arrive(t_dn, t_up, 2)
+    arrive_t(2)
     t_pair(3)
-    arrive(g_dn[0], g_up[0], 2)
+    arrive_g(0, 2)
+    arrive_g(1, 1)
+    arrive_t(3)
+    t_single(1, t_block(4), rk_in, far)
     g_pair(0, 3)
-    arrive(g_dn[1], g_up[1], 2)
-    arrive(t_dn, t_up, 3)
-    t_single(1, zt[4], rk_in, far)
     drain(lall.at[core, pl.ds(0, NX - 1)], x_r)
     logit_pair = remote(lall.at[core], lall.at[core], p_s, p_r, partner)
     logit_pair.start()
-    arrive(g_dn[0], g_up[0], 3)
+    arrive_g(0, 3)
     g_single(0, 1, zg[0, 4], rk_in, far)
+    arrive_g(1, 2)
+    g_single(1, 0, grads[:, 1024:2048], rk_out, z)
     g_pair(1, 1)
     g_pair(1, 2)
     g_pair(1, 3)
-    arrive(g_dn[1], g_up[1], 3)
-    g_single(1, 1, zg[1, 4], rk_in, far)
     drain(lall.at[1 - core], p_r)
 
     valid = iota((1024, 128), 1) < 96
@@ -357,6 +367,8 @@
             tiles.append(jnp.where(here, jnp.broadcast_to(gcol[yy * 8 + zz], (8, 128)), 0.0))
     gate = jnp.sum(jnp.concatenate(tiles, axis=0), axis=1, keepdims=True)
     gate = gate.astype(BF16).astype(F32)
+    arrive_g(1, 3)
+    g_single(1, 1, zg[1, 4], rk_in, far)
 
     def plane(src, dst, send, recv):
         pltpu.make_async_copy(src(me_e), dst, recv).start()
@@ -380,7 +392,6 @@
         cuts.append(
             remote(rt.at[:, :, :, at], pt.at[o], q_s.at[o], q_r.at[o], partner)
         )
-        cuts[-1].start()
 
     def forward(i, carry):
         at = pl.ds(pl.multiple_of(i * 256, 256), 256)
@@ -464,8 +475,10 @@
     for n in range(3):
         lax.fori_loop(n, n + 1, forward, 0)
         ht_copies[n].start()
-        if n == 1:
+        if n == 0:
             scaled(0)
+            for c in cuts:
+                c.start()
     for c in ht_copies:
         c.wait_recv()
     down_half(0)
@@ -541,7 +554,7 @@
         remote(bsend.at[n], ret.at[me_e], ret_s, ret_r, (me_d, to)).start()
 
     pltpu.make_async_copy(bsend.at[where_from(0)[0]], ret.at[me_e], ret_r).start()
-    lax.fori_loop(1, 5, lambda k, c: (send_back(k), c)[1], 0)
+    lax.fori_loop(1, 6, lambda k, c: (send_back(k), c)[1], 0)
     pair_part(1)
     pair_part(3)
     pair_part(0)
@@ -558,7 +571,7 @@
     h3 = g - dens[3] * jnp.sum(g, axis=1, keepdims=True)
     atile[...] = jnp.sum(h3, axis=0, keepdims=True)
     plane(lambda e: atile, abuf.at[me_e], a_s, a_r)
-    lax.fori_loop(5, 16, lambda k, c: (send_back(k), c)[1], 0)
+    lax.fori_loop(6, 19, lambda k, c: (send_back(k), c)[1], 0)
 
     gates_hi = gates.astype(BF16).astype(F32)
     ex_i, ex_j = iota((128, 512), 0), iota((128, 512), 1)
@@ -611,7 +624,7 @@
         h, b = p % 2, p // 2
         rsend[p] = router_t[16 * h : 16 * h + 16, 128 * b : 128 * b + 128].astype(BF16)
     plane(lambda e: rsend.at[e], rrecv.at[me_e], rs_s, rs_r)
-    lax.fori_loop(16, NE, lambda k, c: (send_back(k), c)[1], 0)
+    lax.fori_loop(19, NE, lambda k, c: (send_back(k), c)[1], 0)
     router_in = mm(lgrad, rw[...])
 
     def add_rows(n, rows, terms, out):
@@ -705,7 +718,7 @@
     )
     drain(router_out, o_r)
 
-    for c in t_dn + t_up + g_dn[0] + g_dn[1] + g_up[0] + g_up[1] + ds_copies + y_copies + lg_copies + cuts + half + early + late:
+    for c in t_dn[0] + t_dn[1] + t_up[0] + t_up[1] + g_dn[0] + g_dn[1] + g_up[0] + g_up[1] + ds_copies + y_copies + lg_copies + cuts + half + early + late:
         c.wait_send()
     for c in [logit_pair, pair_copy] + ht_copies:
         c.wait_send()
@@ -745,7 +758,7 @@
             V((4, 2, 16, 1024), BF16), V((2, 4, 2, 16, 512), BF16),
             V((2, NX, NE, 8, 128), F32), V((2, 1024, 128), F32), V((2, 2, 1024, 128), BF16),
             V((24, 128), F32), V((2, 128, 128), F32), V((NE, 1, 128), F32),
-            V((8, TOK, D), BF16), V((2, 8, TOK, 1024), BF16),
+            V((2, 8, TOK, 1024), BF16), V((2, 8, TOK, 1024), BF16),
             V((4, 4, 16, D), BF16), V((2, 4, 4, 16, 1024), BF16),
             V((4, 4, 16, D), BF16), V((4, 4, 16, D), BF16),
             V((4, 4, 4, 16, 256), BF16),
@@ -766,7 +779,7 @@
             V((NE, 16, 128), BF16), V((NE, 16, 128), BF16),
             V((16, 128), BF16), V((ND, 16, 128), BF16), V((16, 128), BF16),
             dma((4,)), dma((3,)),
-            dma((8,)), dma((8,)), dma((2, 8)), dma((2, 8)),
+            dma((2, 8)), dma((2, 8)), dma((2, 8)), dma((2, 8)),
             dma((4, 4)), dma((4, 4)), dma((2, 4, 4)), dma((2, 4, 4)),
             dma((2, 4)), dma((2, 4)), dma((2, 2, 4)), dma((2, 2, 4)),
             dma((8,)), dma((8,)),

time: 87.2 us -> 87.3 us (level)
  no operation moved by 1% of the time
where the time goes in v6:
time: 87.3 us; the launch traced here: 87.2 us
  Pallas kernels  86.5 us (99%)
    pallas_call x1, Pallas kernels, moe(): pl.pallas_call(moe_kernel, name='moe', out_shape=(jax.ShapeDtypeStruct((T...  85.3 us

profile of v6, /device:TPU:1, one launch (start us, length us, event | category | flops | bytes accessed | tf_op | source)
XLA Modules:
  0.0 87.2 jit_solution(17517158230592031931)
XLA Ops:
  0.6 85.3 %moe.1 = (bf16[24,2048]{1,0:T(8,128)(2,1)S(1)}, bf16[256,1536]{1,0:T(8,128)(2,1)S(1)}, bf16[96,2048]{1,0:T(8,128)(2,1)S(1)}, bf16[32,16,128]{2,1,0:T(8,128)(2,1)S(1)}) custom-call(bf16[24,2048]{1,0:T(8,128)(2,1)} %tokens_hbm.1, bf16[24,2048]{1,0:T(8,128)(2,1)} %grads_hbm.1, s32[8,24]{1,0:T(8,128)} %bitcast.4, bf16[32,2048]{1,0:T(8,128)(2,1)} %bitcast.3, ...), custom_call_target="tpu_custom_call" | custom-call | tf_op jit(solution)/shard_map/moe/pallas_call | solution.py:741
  85.9 1.2 %write.1 = (bf16[24,2048]{1,0:T(8,128)(2,1)}, f32[32,2048]{1,0:T(8,128)}, bf16[1,256,768]{2,1,0:T(8,128)(2,1)}, bf16[1,256,768]{2,1,0:T(8,128)(2,1)}, bf16[1,96,2048]{2,1,0:T(8,128)(2,1)}) custom-call(bf16[24,2048]{1,0:T(8,128)(2,1)S(1)} %get-tuple-element.14.gt, bf16[256,1536]{1,0:T(8,128)(2,1)S(1)} %get-tuple-element.15.pair, ...), custom_call_target="tpu_custom_call" | custom-call | tf_op jit(solution)/shard_map/write/pallas_call | solution.py:807

commit v7 on v6

--- a/solution.py
+++ b/solution.py
@@ -540,7 +540,7 @@
         lax.fori_loop(0, 3, one, 0)
 
     pair_part(2)
-    for c in half[4:8]:
+    for c in half[4:8] + early[2:4]:
         c.start()
     for b in range(4):
         at = slice(512 * b, 512 * b + 512)
@@ -606,7 +606,7 @@
             remote(g1.at[1, up], rc1.at[up], n_s.at[2 * n + 4], n_r.at[2 * n + 4], right),
             remote(g1.at[3, down], rd1.at[down], n_s.at[2 * n + 5], n_r.at[2 * n + 5], left),
         ]
-    for c in early[2:6]:
+    for c in early[4:8]:
         c.start()
 
     drain(bbuf, b_r)
@@ -668,7 +668,7 @@
         remote(g1.at[3, pl.ds(128, 128)], rd1.at[pl.ds(128, 128)], m_s.at[5], m_r.at[5], left),
     ]
 
-    for c in late[0:2] + early[6:8]:
+    for c in late[0:2]:
         c.start()
     drain(rrecv, rs_r)
     dsum[...] = jnp.sum(rrecv[...].astype(F32), axis=0).astype(BF16)

time: 87.3 us -> 85.6 us (0.981)
  Pallas kernels: 86.5 us -> 84.8 us
    pallas_call x1, Pallas kernels: 85.3 us -> 83.6 us  [moe(): pl.pallas_call(moe_kernel, name='moe', out_shape=(jax.ShapeDtypeStruct((T...]
where the time goes in v7:
time: 85.6 us; the launch traced here: 85.5 us
  Pallas kernels  84.8 us (99%)
    pallas_call x1, Pallas kernels, moe(): pl.pallas_call(moe_kernel, name='moe', out_shape=(jax.ShapeDtypeStruct((T...  83.6 us

profile of v7, /device:TPU:1, one launch (start us, length us, event | category | flops | bytes accessed | tf_op | source)
XLA Modules:
  0.0 85.5 jit_solution(6096225708726785473)
XLA Ops:
  0.6 83.6 %moe.1 = (bf16[24,2048]{1,0:T(8,128)(2,1)S(1)}, bf16[256,1536]{1,0:T(8,128)(2,1)S(1)}, bf16[96,2048]{1,0:T(8,128)(2,1)S(1)}, bf16[32,16,128]{2,1,0:T(8,128)(2,1)S(1)}) custom-call(bf16[24,2048]{1,0:T(8,128)(2,1)} %tokens_hbm.1, bf16[24,2048]{1,0:T(8,128)(2,1)} %grads_hbm.1, s32[8,24]{1,0:T(8,128)} %bitcast.4, bf16[32,2048]{1,0:T(8,128)(2,1)} %bitcast.3, ...), custom_call_target="tpu_custom_call" | custom-call | tf_op jit(solution)/shard_map/moe/pallas_call | solution.py:741
  84.2 1.2 %write.1 = (bf16[24,2048]{1,0:T(8,128)(2,1)}, f32[32,2048]{1,0:T(8,128)}, bf16[1,256,768]{2,1,0:T(8,128)(2,1)}, bf16[1,256,768]{2,1,0:T(8,128)(2,1)}, bf16[1,96,2048]{2,1,0:T(8,128)(2,1)}) custom-call(bf16[24,2048]{1,0:T(8,128)(2,1)S(1)} %get-tuple-element.14.gt, bf16[256,1536]{1,0:T(8,128)(2,1)S(1)} %get-tuple-element.15.pair, ...), custom_call_target="tpu_custom_call" | custom-call | tf_op jit(solution)/shard_map/write/pallas_call | solution.py:807
